TPU v7x, 128 devices: a whole 4x4x4 slice. The times are simulated.
128 devices in a mesh: dp: 8 (over z, core), table: 16 (over x, y).
Axes of the slice: x: 4, y: 4, z: 4, core: 2. Of those that a mesh axis runs over, the one named last changes fastest.
Arguments:
- table: bfloat16 [65536, 512], P('table'), may hold values from -6 to 6
- w_in: bfloat16 [512, 2048], replicated, may hold values from -0.25 to 0.25
- w_out: bfloat16 [512, 512], replicated, may hold values from -0.25 to 0.25
- owner: int32 [131072, 2], P(('dp', 'table')), may hold values from 0 to 15, all different within a row; in each aligned block of 1024 rows (0 to 1023, 1024 to 2047, ...) at most 256 rows name the same one
- local_row: int32 [131072, 2], P(('dp', 'table')), may hold values from 0 to 4095
- doc_ids: int32 [128, 1024], P(('dp', 'table')), may hold values from 0 to 3, never falling along the last dimension, each value on 1 to 768 neighbouring positions
- out_grad: bfloat16 [131072, 512], P(('dp', 'table')), may hold values from -6 to 6
Outputs:
- layer_out: bfloat16 [131072, 512], P(('dp', 'table'))
- grad_w_in: float32 [512, 2048], replicated
- grad_w_out: float32 [512, 512], replicated
- grad_table: float32 [65536, 512], P('table', 'dp')
Inputs may be any that keep to these rules, and one draw needn't show every extreme that they name: The 2 owners of one event differ; among the events of one block of 1024, no owner is named by more than 256 lookups. `doc_ids`: along a row the ids never fall; every id of 0 to 3 covers 1 to 768 events.
All inputs are finite; a program needn't handle non-finite values.
Results may differ from a plain program's by a relative error of at most 0.014.
Values may be sent and summed in bfloat16 or wider, within the bound.
No kernel may reach another device: no remote copies, remote signals or barrier semaphores. Data moves between devices by JAX's collectives and lax.ppermute only.
A program may use at most 128 MiB of HBM per device.

v0:
```python
import jax
import jax.numpy as jnp
from jax import lax
from jax.sharding import PartitionSpec as P

HEADS = 4
MAXLEN = 768


def normalize(values):
    center = values - jnp.mean(values, axis=-1, keepdims=True)
    spread = jnp.mean(center * center, axis=-1, keepdims=True)
    return center * lax.rsqrt(spread + 1e-06)


def hstu_layer(inputs, w_in, w_out, segment):
    length, width = inputs.shape
    head_dim = width // HEADS
    widened = inputs.astype(jnp.float32)
    normed = normalize(widened).astype(jnp.bfloat16)
    projected = jax.nn.silu(jnp.dot(normed, w_in, preferred_element_type=jnp.float32)).astype(
        jnp.bfloat16
    )
    gate_part, value_part, query_part, key_part = jnp.split(projected, 4, axis=1)
    query_heads = query_part.reshape(length, HEADS, head_dim)
    key_heads = key_part.reshape(length, HEADS, head_dim)
    value_heads = value_part.reshape(length, HEADS, head_dim)
    scores = jnp.einsum(
        "thd,shd->hts", query_heads, key_heads, preferred_element_type=jnp.float32
    ) * head_dim ** (-0.5)
    row_index = lax.broadcasted_iota(jnp.int32, (length, length), 0)
    col_index = lax.broadcasted_iota(jnp.int32, (length, length), 1)
    allowed = (segment[:, None] == segment[None, :]) & (row_index >= col_index)
    weights = (jnp.where(allowed[None], jax.nn.silu(scores), 0.0) / MAXLEN).astype(jnp.bfloat16)
    mixed = jnp.einsum(
        "hts,shd->thd", weights, value_heads, preferred_element_type=jnp.float32
    ).reshape(length, width)
    gated = (normalize(mixed) * gate_part.astype(jnp.float32)).astype(jnp.bfloat16)
    return (widened + jnp.dot(gated, w_out, preferred_element_type=jnp.float32)).astype(
        jnp.bfloat16
    )


def shards(table, w_in, w_out, owner, local_row, doc_ids, out_grad):
    events, lookups_each = owner.shape
    width = table.shape[1]
    rows_owned = table.shape[0]
    owners = lax.axis_size("table")
    capacity = 2 * events * lookups_each // owners
    lookups = events * lookups_each
    flat_owner = owner.reshape(lookups)
    flat_local = local_row.reshape(lookups)
    member = (flat_owner[:, None] == jnp.arange(owners, dtype=jnp.int32)[None, :]).astype(jnp.int32)
    position = jnp.sum(jnp.cumsum(member, axis=0) * member, axis=1) - 1
    slot_index = flat_owner * capacity + position
    requests = (
        jnp.zeros((owners * capacity,), jnp.int32)
        .at[slot_index]
        .set(flat_local)
        .reshape(owners, capacity)
    )
    found = jnp.take(
        table, lax.all_to_all(requests, "table", split_axis=0, concat_axis=0, tiled=True), axis=0
    )
    arrived = lax.all_to_all(found, "table", split_axis=0, concat_axis=0, tiled=True)
    picked = jnp.take(arrived.reshape(owners * capacity, width), slot_index, axis=0)
    embedded = jnp.sum(
        picked.astype(jnp.float32).reshape(events, lookups_each, width), axis=1
    ).astype(jnp.bfloat16)
    segment = doc_ids[0]

    def forward(first, second, third):
        return hstu_layer(first, second, third, segment)

    layer_out, pullback = jax.vjp(forward, embedded, w_in, w_out)
    embed_grad, grad_first, grad_second = pullback(out_grad)
    grad_w_in, grad_w_out = lax.psum(
        (grad_first.astype(jnp.float32), grad_second.astype(jnp.float32)), ("dp", "table")
    )
    per_lookup = jnp.broadcast_to(embed_grad[:, None, :], (events, lookups_each, width)).reshape(
        lookups, width
    )
    sending = (
        jnp.zeros((owners * capacity, width), jnp.bfloat16)
        .at[slot_index]
        .set(per_lookup)
        .reshape(owners, capacity, width)
    )
    received, received_ids = (
        lax.all_to_all(sending, "table", split_axis=0, concat_axis=0, tiled=True),
        lax.all_to_all(requests, "table", split_axis=0, concat_axis=0, tiled=True),
    )
    summed = jax.ops.segment_sum(
        received.reshape(owners * capacity, width).astype(jnp.float32),
        received_ids.reshape(-1),
        num_segments=rows_owned,
    )
    grad_table = lax.psum_scatter(
        summed.astype(jnp.bfloat16), "dp", scatter_dimension=1, tiled=True
    ).astype(jnp.float32)
    return (layer_out, grad_w_in, grad_w_out, grad_table)


def solution(mesh):
    placed = (
        P("table", None),
        P(),
        P(),
        P(("dp", "table"), None),
        P(("dp", "table"), None),
        P(("dp", "table"), None),
        P(("dp", "table"), None),
    )
    return jax.shard_map(
        shards,
        mesh=mesh,
        in_specs=placed,
        out_specs=(P(("dp", "table"), None), P(), P(), P("table", "dp")),
        check_vma=False,
    )
```

profile of v0, /device:TPU:1, one launch (start us, length us, event | category | flops | bytes accessed | tf_op | source)
XLA Modules:
  0.0 539.1 jit_solution(17196248832249425726)
XLA Ops:
  10.3 4.5 reduce-window.6
  17.4 8.1 %scatter_custom_fusion = s32[4096]{0:T(1024)S(1)} fusion(s32[2048]{0:T(1024)S(1)} %bitcast.117, s32[2048]{0:T(1024)S(1)} %reshape.282, s32[]{:T(128)} %constant.61.clone.1), kind=kCustom, calls=%fused_computation.88 | custom fusion | bytes 16388 | tf_op jit(solution)/shard_map/scatter | solution.py:59
  25.5 13.8 %all_to_all.26 = s32[16,1,256]{2,1,0:T(1,128)S(1)} all-to-all(s32[16,1,256]{2,1,0:T(1,128)S(1)} %bitcast.115), channel_id=1, replica_groups=mesh['dp'=8,'table'=16] {'table'}, dimensions={0} | all-to-all | bytes 32768 | tf_op jit(solution)/shard_map/all_to_all | solution.py:63
  39.4 20.2 %gather_fusion = bf16[4096,512]{1,0:T(8,128)(2,1)} fusion(bf16[4096,512]{1,0:T(8,128)(2,1)} %param.7, s32[4096]{0:T(1024)S(1)} %broadcast_clamp_fusion), kind=kCustom, calls=%fused_computation | custom fusion | bytes 8404992 | tf_op jit(solution)/shard_map/jit(_take)/gather | solution.py:62
  59.6 4.0 broadcast_select_fusion
  63.5 4.7 all-to-all-start.1
  71.3 48.7 %all-to-all-done.1 = bf16[16,256,512]{2,1,0:T(8,128)(2,1)} async-done(((bf16[16,256,512]{2,1,0:T(8,128)(2,1)}), bf16[16,256,512]{2,1,0:T(8,128)(2,1)}, u32[]{:S(2)}, u32[]{:S(2)}) %all-to-all-start.1) | async-done | bytes 4194336 | tf_op jit(solution)/shard_map/all_to_all | solution.py:65
  120.0 12.0 %gather_fusion.1 = bf16[2048,512]{1,0:T(8,128)(2,1)} fusion(bf16[4096,512]{1,0:T(8,128)(2,1)} %bitcast.7, s32[2048]{0:T(1024)S(1)} %broadcast_clamp_fusion.1), kind=kCustom, calls=%fused_computation.1 | custom fusion | bytes 4202496 | tf_op jit(solution)/shard_map/jit(_take)/gather | solution.py:66
  132.0 4.1 gather.12
  136.1 9.6 %fusion.20 = bf16[1024,512]{1,0:T(8,128)(2,1)S(1)} fusion(bf16[1024,2,512]{2,1,0:T(2,128)(2,1)} %gather.12, pred[1024,2]{1,0:T(8,128)(4,1)S(1)} %copy.68), kind=kLoop, calls=%fused_computation.46 | loop fusion | flops 1572864 | bytes 3147776 | tf_op jit(solution)/shard_map/reduce_sum | solution.py:67
  146.5 5.7 %multiply_convert_fusion.1 = (bf16[1024,2048]{1,0:T(8,128)(2,1)S(1)}, f32[1024,2048]{1,0:T(8,128)}) fusion(bf16[512,2048]{1,0:T(8,128)(2,1)S(1)} %copy-done, bf16[1024,512]{1,0:T(8,128)(2,1)S(1)} %fusion.20, f32[1024]{0:T(1024)S(1)} %fusion.41, f32[1024]{0:T(1024)S(1)} %broadcast_multiply_fusion.2), kind=kOutput, calls=%fused_computation.18 | convolution fusion | flops 2160066560 | bytes 15736832 | tf_op jit(solution)/shard_map/jvp()/dot_general | solution.py:21
  160.6 12.3 %multiply_convert_fusion = (bf16[4,1024,1024]{2,1,0:T(8,128)(2,1)S(1)}, f32[4,1024,1024]{2,1,0:T(8,128)}) fusion(pred[1024,1024]{1,0:T(8,128)(4,1)} %fusion.8, bf16[1024,4,128]{0,2,1:T(8,128)(2,1)} %bitcast.105, bf16[1024,4,128]{0,2,1:T(8,128)(2,1)} %bitcast.107), kind=kOutput, calls=%fused_computation.9 | convolution fusion | flops 1107296256 | bytes 28311552 | tf_op jit(solution)/shard_map/jvp(thd,shd->hts)/dot_general | solution.py:28
  177.7 2.9 copy.89
  180.7 3.4 multiply_reduce_fusion
  184.1 3.4 fusion.46
  187.5 6.1 %fusion.28 = bf16[4,128,1024]{2,1,0:T(8,128)(2,1)} fusion(bf16[4,1024,1024]{2,1,0:T(8,128)(2,1)} %copy-done.1, f32[1024,512]{1,0:T(8,128)S(1)} %get-tuple-element.19, f32[1024]{0:T(1024)S(1)} %negate_multiply_fusion.1), kind=kOutput, calls=%fused_computation.60 | convolution fusion | flops 1074790400 | bytes 11538432 | tf_op jit(solution)/shard_map/transpose(jvp(hts,shd->thd))/dot_general | solution.py:35
  193.6 15.0 %fusion.2 = bf16[4,1024,1024]{2,1,0:T(8,128)(2,1)} fusion(f32[4,1024,1024]{2,1,0:T(8,128)} %get-tuple-element.30, pred[1024,1024]{1,0:T(8,128)(4,1)S(1)} %copy-done.10, bf16[128,4,8,128]{3,2,1,0:T(8,128)(2,1)S(1)} %copy-done.9, f32[1024,512]{1,0:T(8,128)S(1)} %get-tuple-element.19, f32[1024]{0:T(1024)S(1)} %negate_multiply_fusion.1), kind=kOutput, calls=%fused_computation.8 | convolution fusion | flops 1137704960 | bytes 29364224 | tf_op jit(solution)/shard_map/transpose(jvp(hts,shd->thd))/dot_general | solution.py:35
  208.7 7.3 %fusion.49 = bf16[4,1024,128]{1,2,0:T(8,128)(2,1)} fusion(bf16[4,1024,1024]{2,1,0:T(8,128)(2,1)} %fusion.2, bf16[1024,4,128]{0,2,1:T(8,128)(2,1)S(1)} %bitcast.108), kind=kOutput, calls=%fused_computation.107 | convolution fusion | flops 1073741824 | bytes 10485760 | tf_op jit(solution)/shard_map/transpose(jvp(thd,shd->hts))/dot_general | solution.py:28
  216.0 5.7 %fusion.48 = bf16[4,1024,128]{1,2,0:T(8,128)(2,1)} fusion(bf16[4,1024,1024]{2,1,0:T(8,128)(2,1)} %fusion.2, bf16[1024,4,128]{0,2,1:T(8,128)(2,1)S(1)} %bitcast.106), kind=kOutput, calls=%fused_computation.106 | convolution fusion | flops 1073741824 | bytes 10485760 | tf_op jit(solution)/shard_map/transpose(jvp(thd,shd->hts))/dot_general | solution.py:28
  228.6 6.5 %fusion.3 = bf16[1024,2048]{1,0:T(8,128)(2,1)S(1)} fusion(f32[1024,2048]{1,0:T(8,128)} %get-tuple-element.28, bf16[1024,512]{1,0:T(8,128)(2,1)} %copy.94, bf16[1024,512]{1,0:T(8,128)(2,1)} %copy.93, bf16[1024,512]{1,0:T(8,128)(2,1)} %copy.92, bf16[1024,512]{1,0:T(8,128)(2,1)} %get-tuple-element.24), kind=kLoop, calls=%fused_computation.14 | loop fusion | flops 37748736 | bytes 16777216 | tf_op jit(solution)/shard_map/transpose(jvp(jit(silu)))/add_any | solution.py:21
  242.1 4.1 reshape.290
  246.2 12.8 %scatter_custom_fusion.1 = bf16[4096,512]{1,0:T(8,128)(2,1)} fusion(s32[2048]{0:T(1024)S(1)} %bitcast.119, bf16[2048,512]{1,0:T(8,128)(2,1)} %reshape.290, bf16[]{:T(256)} %constant.66.clone.1), kind=kCustom, calls=%fused_computation.53 | custom fusion | bytes 4194816 | tf_op jit(solution)/shard_map/scatter | solution.py:86
  259.0 51.2 %all_to_all.27 = bf16[16,256,512]{2,1,0:T(8,128)(2,1)} all-to-all(bf16[16,256,512]{2,1,0:T(8,128)(2,1)} %bitcast.102), channel_id=1, replica_groups=mesh['dp'=8,'table'=16] {'table'}, dimensions={0} | all-to-all | bytes 8388608 | tf_op jit(solution)/shard_map/all_to_all | solution.py:90
  310.2 32.1 %scatter_custom_fusion.2 = f32[4096,512]{1,0:T(8,128)} fusion(s32[4096]{0:T(1024)S(1)} %bitcast.113, bf16[4096,512]{1,0:T(8,128)(2,1)} %bitcast.103, f32[]{:T(128)} %constant.67.clone.1), kind=kCustom, calls=%fused_computation.16 | custom fusion | flops 4194304 | bytes 12582916 | tf_op jit(solution)/shard_map/scatter-add | solution.py:93
  342.3 5.9 %convert_element_type.131 = bf16[4096,512]{1,0:T(8,128)(2,1)} convert(f32[4096,512]{1,0:T(8,128)} %scatter_custom_fusion.2) | non-fusion elementwise | flops 2097152 | bytes 12582912 | tf_op jit(solution)/shard_map/convert_element_type | solution.py:99
  348.2 6.4 %copy.95 = bf16[4096,512]{0,1:T(8,128)(2,1)} copy(bf16[4096,512]{1,0:T(8,128)(2,1)} %convert_element_type.131) | data formatting | bytes 8388608
  355.0 3.4 fusion.30
  358.4 4.6 fusion.13
  363.1 3.0 fusion.19
  366.1 30.3 %reduce-scatter.4.cloned.1.call-done = bf16[64,4096]{1,0:T(8,128)(2,1)} async-done(((bf16[512,4096]{1,0:T(8,128)(2,1)}), bf16[64,4096]{1,0:T(8,128)(2,1)}) %reduce-scatter.4.cloned.1.call-update) | async-done | bytes 524304
  399.2 126.2 %all-reduce.3.cloned.1.call-done = (f32[512,2048]{1,0:T(8,128)}, f32[512,512]{1,0:T(8,128)}) async-done(((f32[512,2048]{1,0:T(8,128)}, f32[512,512]{1,0:T(8,128)}), (f32[512,2048]{1,0:T(8,128)}, f32[512,512]{1,0:T(8,128)})) %all-reduce.3.cloned.1.call-update) | async-done | bytes 5242896 | tf_op jit(solution)/shard_map/psum | solution.py:77
  525.4 4.8 copy.129
  (84 shorter events, 40.0 us)
Async XLA Ops:
  8.0 138.5 %copy-start = (bf16[512,2048]{1,0:T(8,128)(2,1)S(1)}, bf16[512,2048]{1,0:T(8,128)(2,1)}, u32[]{:S(2)}) copy-start(bf16[512,2048]{1,0:T(8,128)(2,1)} %param.8) | copy-start | bytes 6291460
  63.5 5.9 %copy-start.14 = (s32[1024,2]{0,1:T(2,128)S(1)}, s32[1024,2]{0,1:T(2,128)}, u32[]{:S(2)}) copy-start(s32[1024,2]{0,1:T(2,128)} %param.10) | copy-start | bytes 24580
  63.5 6.3 %copy-start.15 = (s32[1,1024]{1,0:T(1,128)S(1)}, s32[1,1024]{1,0:T(1,128)}, u32[]{:S(2)}) copy-start(s32[1,1024]{1,0:T(1,128)} %param.12) | copy-start | bytes 12292
  63.5 56.5 %all-to-all-start.1 = ((bf16[16,256,512]{2,1,0:T(8,128)(2,1)}), bf16[16,256,512]{2,1,0:T(8,128)(2,1)}, u32[]{:S(2)}, u32[]{:S(2)}) async-start(bf16[16,256,512]{2,1,0:T(8,128)(2,1)} %broadcast_select_fusion), calls=%async_computation.1 | async-start | bytes 8388608 | tf_op jit(solution)/shard_map/all_to_all | solution.py:65
  68.2 328.2 %reduce-scatter.4.cloned.1.call-start = ((), (), s32[]{:S(2)}) async-start(), calls=%async_computation.4 | async-start | bytes 4718592
  152.2 2.0 copy-start.6
  160.6 12.3 %copy-start.8 = (bf16[128,4,8,128]{3,2,1,0:T(8,128)(2,1)S(1)}, bf16[128,4,8,128]{3,2,1,0:T(8,128)(2,1)}, u32[]{:S(2)}) copy-start(bf16[128,4,8,128]{3,2,1,0:T(8,128)(2,1)} %get-tuple-element.21) | copy-start | bytes 3145732
  172.9 3.2 copy-start.1
  176.1 1.3 copy-start.5
  180.7 3.4 copy-start.4
  187.5 6.1 %copy-start.9 = (bf16[128,4,8,128]{3,2,1,0:T(8,128)(2,1)S(1)}, bf16[128,4,8,128]{3,2,1,0:T(8,128)(2,1)}, u32[]{:S(2)}) copy-start(bf16[128,4,8,128]{3,2,1,0:T(8,128)(2,1)} %get-tuple-element.21) | copy-start | bytes 3145732
  187.5 6.1 %copy-start.10 = (pred[1024,1024]{1,0:T(8,128)(4,1)S(1)}, pred[1024,1024]{1,0:T(8,128)(4,1)}, u32[]{:S(2)}) copy-start(pred[1024,1024]{1,0:T(8,128)(4,1)} %fusion.8) | copy-start | bytes 3145732
  193.6 15.0 %copy-start.12 = (bf16[1024,512]{0,1:T(8,128)(2,1)S(1)}, bf16[1024,512]{0,1:T(8,128)(2,1)}, u32[]{:S(2)}) copy-start(bf16[1024,512]{0,1:T(8,128)(2,1)} %copy.99) | copy-start | bytes 3145732
  208.7 7.4 %copy-start.11 = (bf16[1024,512]{0,1:T(8,128)(2,1)S(1)}, bf16[1024,512]{0,1:T(8,128)(2,1)}, u32[]{:S(2)}) copy-start(bf16[1024,512]{0,1:T(8,128)(2,1)} %copy.98) | copy-start | bytes 3145732
  235.1 2.5 copy-start.2
  235.1 3.5 copy-start.7
  354.6 170.8 %all-reduce.3.cloned.1.call-start = ((), (), s32[]{:S(2)}) async-start(), calls=%async_computation.5 | async-start | bytes 10485760 | tf_op jit(solution)/shard_map/psum | solution.py:77
  355.0 3.4 copy-start.3
  525.4 4.8 copy-start.13
Sparse Core Ops, SparseCore 0:
  354.8 41.5 reduce-scatter.3
Sparse Core Ops, SparseCore 1:
  363.1 162.2 all-reduce.2
where the time goes:
time: 544 us; the launch traced here: 539 us
  waiting for transfers between devices  205 us (38%)
  local copies, waits for them, and re-layouts  103 us (19%)
  other arithmetic  71.9 us (13%)
  matrix products  71.9 us (13%)
  blocking collectives  65 us (12%)
  between operations  16.3 us (3%)
  starting transfers between devices  5.57 us (1%)
    psum x1, waiting for transfers between devices, shards(): lax.psum((grad_first.astype(jnp.float32), grad_second.astype(jnp.float32)...  126 us
    all_to_all x1, blocking collectives, shards(): lax.all_to_all(sending, 'table', split_axis=0, concat_axis=0, tiled=True)  51.2 us
    all_to_all x1, waiting for transfers between devices, shards(): lax.all_to_all(found, 'table', split_axis=0, concat_axis=0, tiled=True)  48.7 us
    scatter-add x1, other arithmetic, shards(): jax.ops.segment_sum(received.reshape(owners * capacity, width).astype(jnp...  32.1 us
    unnamed x3, waiting for transfers between devices  30.3 us
    dot_general x3, matrix products, hstu_layer(): jnp.einsum('thd,shd->hts', query_heads, key_heads, preferred_element_type...  25.3 us
    dot_general x3, matrix products, hstu_layer(): jnp.einsum('hts,shd->thd', weights, value_heads, preferred_element_type=j...  24 us
    unnamed x40, local copies, waits for them, and re-layouts  22.5 us
  transfers between devices with their start and end apart: 3, of which 3 were waited for; matrix products, arithmetic and copies ran while one was open for 3% of the time, Pallas kernels for 0%

commit v1 on v0

v1 whole, which is shorter than its diff:
```python
import jax
import jax.numpy as jnp
from jax import lax
from jax.experimental import pallas as pl
from jax.experimental.pallas import tpu as pltpu
from jax.sharding import PartitionSpec as P


HEADS = 4
MAXLEN = 768
EPS = 1e-06
BF = jnp.bfloat16
F32 = jnp.float32
NN = (((1,), (0,)), ((), ()))
NT = (((1,), (1,)), ((), ()))
TN = (((0,), (0,)), ((), ()))


def dot(a, b, dims=NN):
    return lax.dot_general(a, b, dims, preferred_element_type=F32)


def iota(shape, dim):
    return lax.broadcasted_iota(jnp.int32, shape, dim)


def onehot(cond):
    return jnp.where(cond, 1.0, 0.0).astype(BF)


def route_kernel(own_ref, loc_ref, slot_ref, req_ref, *, owners, capacity, dummy):
    own = own_ref[...]
    loc = loc_ref[...]
    rows, lanes = own.shape
    member = jnp.concatenate([onehot(own == o) for o in range(owners)], axis=0)
    total = owners * rows
    upper = onehot(iota((lanes, lanes), 0) <= iota((lanes, lanes), 1))
    inside = dot(member, upper)
    left = iota((total, total), 0)
    right = iota((total, total), 1)
    before = onehot((left // rows == right // rows) & (right < left))
    offset = jnp.sum(dot(before, member), axis=1, keepdims=True)
    place = (inside + offset - 1.0) * member.astype(F32)
    position = place[0:rows]
    for o in range(1, owners):
        position = position + place[o * rows : (o + 1) * rows]
    position = position.astype(jnp.int32)
    slot_ref[...] = own * capacity + position
    who = iota((owners, lanes), 0)
    where = iota((capacity, lanes), 0)
    found = jnp.zeros((3 * owners, capacity), F32)
    for r in range(rows):
        mine = own[r : r + 1, :] == who
        row = loc[r : r + 1, :]
        high = jnp.where(mine, (row >> 8).astype(F32), 0.0).astype(BF)
        low = jnp.where(mine, (row & 255).astype(F32), 0.0).astype(BF)
        left_side = jnp.concatenate([high, low, onehot(mine)], axis=0)
        found = found + dot(left_side, onehot(position[r : r + 1, :] == where), NT)
    high = found[0:owners].astype(jnp.int32)
    low = found[owners : 2 * owners].astype(jnp.int32)
    used = found[2 * owners :] > 0.5
    req_ref[...] = jnp.where(used, high * 256 + low, dummy)


def gather_kernel(ids_ref, table_ref, out_ref, wide, picked):
    step = pl.program_id(0)
    count, width = out_ref.shape
    rows = table_ref.shape[0]
    parts = width // 128
    chunk = 64

    @pl.when(step == 0)
    def _():
        def widen(i, carry):
            base = pl.multiple_of(i * chunk, chunk)
            for c in range(parts):
                wide[pl.ds(base * parts + c, chunk, stride=parts), :] = table_ref[
                    pl.ds(base, chunk), c * 128 : (c + 1) * 128
                ].astype(F32)
            return carry

        lax.fori_loop(0, rows // chunk, widen, 0)
        wide[rows * parts : rows * parts + 8, :] = jnp.zeros((8, 128), F32)

    def copy_rows(k, carry):
        for u in range(16):
            s = k * 16 + u
            row = ids_ref[step * count + s]
            picked[pl.ds(pl.multiple_of(s * parts, parts), parts), :] = wide[
                pl.ds(pl.multiple_of(row * parts, parts), parts), :
            ]
        return carry

    lax.fori_loop(0, count // 16, copy_rows, 0)
    for c in range(parts):
        out_ref[:, c * 128 : (c + 1) * 128] = picked[pl.ds(c, count, stride=parts), :].astype(BF)


def scatter_kernel(ids_ref, cnt_ref, grad_ref, out_ref, even, odd, rows_in):
    step = pl.program_id(0)
    count, width = grad_ref.shape
    parts = width // 128
    rows = out_ref.shape[1]

    @pl.when(step == 0)
    def _():
        def clear(i, carry):
            base = pl.ds(pl.multiple_of(i * 128, 128), 128)
            even[base, :] = jnp.zeros((128, 128), F32)
            odd[base, :] = jnp.zeros((128, 128), F32)
            return carry

        lax.fori_loop(0, rows * parts // 128, clear, 0)

    for c in range(parts):
        rows_in[pl.ds(c, count, stride=parts), :] = grad_ref[:, c * 128 : (c + 1) * 128].astype(F32)

    def add_rows(k, carry):
        for u in range(8):
            s = k * 8 + u
            row = ids_ref[step * count + s]
            total = odd if u % 2 else even
            at = pl.ds(pl.multiple_of(row * parts, parts), parts)
            total[at, :] = (
                total[at, :] + rows_in[pl.ds(pl.multiple_of(s * parts, parts), parts), :]
            )
        return carry

    lax.fori_loop(0, (cnt_ref[step] + 7) // 8, add_rows, 0)

    @pl.when(step == pl.num_programs(0) - 1)
    def _():
        def flush(i, carry):
            for c in range(parts):
                at = pl.ds(i * (128 * parts) + c, 128, stride=parts)
                both = even[at, :] + odd[at, :]
                out_ref[c * 128 : (c + 1) * 128, pl.ds(pl.multiple_of(i * 128, 128), 128)] = (
                    both.T.astype(BF)
                )
            return carry

        lax.fori_loop(0, rows // 128, flush, 0)


def normal(values):
    center = values - jnp.mean(values, axis=-1, keepdims=True)
    spread = jnp.mean(center * center, axis=-1, keepdims=True)
    scale = lax.rsqrt(spread + EPS)
    return center * scale, scale


def normal_back(grad, unit, scale):
    shared = jnp.mean(grad, axis=-1, keepdims=True)
    along = jnp.mean(grad * unit, axis=-1, keepdims=True)
    return scale * (grad - shared - unit * along)


def layer_kernel(
    arrived_ref,
    slot_ref,
    w_in_ref,
    w_out_ref,
    doc_ref,
    og_ref,
    out_ref,
    sending_ref,
    normed_ref,
    du_ref,
    gated_ref,
    emb_ref,
    proj_ref,
    wts_ref,
    dws_ref,
    mixed_ref,
    dmix_ref,
    eg_ref,
):
    events, width = og_ref.shape
    slots = arrived_ref.shape[0]
    head = width // HEADS
    blk = 256
    nblk = events // blk
    lane_rows = events // 128
    cap_step = 256
    slot_all = slot_ref[...]
    slot_cols = slot_all.astype(F32).T.astype(jnp.int32)
    doc_rows = doc_ref[...]
    doc_cols = jnp.broadcast_to(doc_rows.astype(F32), (8, events)).T[:, 0:1].astype(jnp.int32)
    scale = head ** (-0.5)

    for b in range(nblk):
        rows = slice(b * blk, (b + 1) * blk)
        per = blk // 128
        first = jnp.concatenate(
            [slot_cols[:, b * per + i : b * per + i + 1] for i in range(per)], axis=0
        )
        second = jnp.concatenate(
            [slot_cols[:, lane_rows + b * per + i : lane_rows + b * per + i + 1] for i in range(per)],
            axis=0,
        )
        total = jnp.zeros((blk, width), F32)
        for o in range(slots // cap_step):
            where = iota((blk, cap_step), 1) + o * cap_step
            pick = onehot((where == first) | (where == second))
            total = total + dot(pick, arrived_ref[o * cap_step : (o + 1) * cap_step, :])
        embedded = total.astype(BF)
        emb_ref[rows, :] = embedded
        unit, _ = normal(embedded.astype(F32))
        normed = unit.astype(BF)
        normed_ref[rows, :] = normed
        for c in range(4):
            cols = slice(c * width, (c + 1) * width)
            u = dot(normed, w_in_ref[:, cols])
            sig = 0.5 * jnp.tanh(0.5 * u) + 0.5
            act = u * sig
            proj_ref[rows, cols] = act.astype(BF)
            du_ref[rows, cols] = (sig + act * (1.0 - sig)).astype(BF)

    def heads_forward(h, carry):
        def cols(part):
            return pl.ds(pl.multiple_of(part * width + h * head, head), head)

        mine = pl.ds(pl.multiple_of(h * head, head), head)
        for i in range(nblk):
            rows = slice(i * blk, (i + 1) * blk)
            query = proj_ref[rows, cols(2)]
            total = jnp.zeros((blk, head), F32)
            for j in range(i + 1):
                keys = slice(j * blk, (j + 1) * blk)
                scores = dot(query, proj_ref[keys, cols(3)], NT) * scale
                allowed = doc_cols[rows] == doc_rows[:, keys]
                if i == j:
                    allowed = allowed & (iota((blk, blk), 0) >= iota((blk, blk), 1))
                sig = 0.5 * jnp.tanh(0.5 * scores) + 0.5
                act = scores * sig
                weight = jnp.where(allowed, act * (1.0 / MAXLEN), 0.0).astype(BF)
                slope = sig + act * (1.0 - sig)
                wts_ref[h, rows, keys] = weight
                dws_ref[h, rows, keys] = jnp.where(allowed, slope * (scale / MAXLEN), 0.0).astype(BF)
                total = total + dot(weight, proj_ref[keys, cols(1)])
            mixed_ref[rows, mine] = total
        return carry

    lax.fori_loop(0, HEADS, heads_forward, 0)

    for b in range(nblk):
        rows = slice(b * blk, (b + 1) * blk)
        unit, spread = normal(mixed_ref[rows, :])
        gate = proj_ref[rows, 0:width].astype(F32)
        gated = (unit * gate).astype(BF)
        gated_ref[rows, :] = gated
        out_ref[rows, :] = (emb_ref[rows, :].astype(F32) + dot(gated, w_out_ref[...])).astype(BF)
        dgated = dot(og_ref[rows, :], w_out_ref[...], NT).astype(BF).astype(F32)
        dmix_ref[rows, :] = normal_back(dgated * gate, unit, spread).astype(BF)
        dgate = (dgated * unit).astype(BF).astype(F32)
        du_ref[rows, 0:width] = (dgate * du_ref[rows, 0:width].astype(F32)).astype(BF)

    def heads_backward(h, carry):
        def cols(part):
            return pl.ds(pl.multiple_of(part * width + h * head, head), head)

        mine = pl.ds(pl.multiple_of(h * head, head), head)

        def put(rows, part, value):
            at = cols(part)
            du_ref[rows, at] = (
                value.astype(BF).astype(F32) * du_ref[rows, at].astype(F32)
            ).astype(BF)

        for j in range(nblk):
            keys = slice(j * blk, (j + 1) * blk)
            value = proj_ref[keys, cols(1)]
            dkey = jnp.zeros((blk, head), F32)
            dvalue = jnp.zeros((blk, head), F32)
            for i in range(j, nblk):
                rows = slice(i * blk, (i + 1) * blk)
                dmix = dmix_ref[rows, mine]
                dscore = (
                    dot(dmix, value, NT) * dws_ref[h, rows, keys].astype(F32)
                ).astype(BF)
                dws_ref[h, rows, keys] = dscore
                dvalue = dvalue + dot(wts_ref[h, rows, keys], dmix, TN)
                dkey = dkey + dot(dscore, proj_ref[rows, cols(2)], TN)
            put(keys, 1, dvalue)
            put(keys, 3, dkey)
        for i in range(nblk):
            rows = slice(i * blk, (i + 1) * blk)
            upto = slice(0, (i + 1) * blk)
            put(rows, 2, dot(dws_ref[h, rows, upto], proj_ref[upto, cols(3)]))
        return carry

    lax.fori_loop(0, HEADS, heads_backward, 0)

    for b in range(nblk):
        rows = slice(b * blk, (b + 1) * blk)
        dnormed = dot(du_ref[rows, :], w_in_ref[...], NT).astype(BF).astype(F32)
        unit, spread = normal(emb_ref[rows, :].astype(F32))
        grad = normal_back(dnormed, unit, spread) + og_ref[rows, :].astype(F32)
        eg_ref[rows, :] = grad.astype(BF)

    for o in range(slots // cap_step):
        where = iota((cap_step, 128), 0) + o * cap_step
        picks = [
            onehot(
                (where == slot_all[r : r + 1, :])
                | (where == slot_all[lane_rows + r : lane_rows + r + 1, :])
            )
            for r in range(lane_rows)
        ]
        pick = jnp.concatenate(picks, axis=1)
        sending_ref[o * cap_step : (o + 1) * cap_step, :] = dot(pick, eg_ref[...]).astype(BF)


def weights_kernel(normed_ref, du_ref, gated_ref, og_ref, out_ref):
    width = gated_ref.shape[1]
    wide = du_ref.shape[1]
    for c in range(wide // width):
        cols = slice(c * width, (c + 1) * width)
        out_ref[:, cols] = dot(normed_ref[...], du_ref[:, cols], TN).astype(BF)
    out_ref[:, wide:] = dot(gated_ref[...], og_ref[...], TN).astype(BF)


def params(mib, **more):
    return pltpu.CompilerParams(vmem_limit_bytes=mib * 2**20, **more)


def route(own, loc, capacity, owners, dummy):
    return pl.pallas_call(
        lambda *refs: route_kernel(*refs, owners=owners, capacity=capacity, dummy=dummy),
        out_shape=(
            jax.ShapeDtypeStruct(own.shape, jnp.int32),
            jax.ShapeDtypeStruct((owners, capacity), jnp.int32),
        ),
        name="route",
    )(own, loc)


def gather_rows(ids, table, owners, capacity):
    rows, width = table.shape
    parts = width // 128
    return pl.pallas_call(
        gather_kernel,
        out_shape=jax.ShapeDtypeStruct((owners * capacity, width), BF),
        grid_spec=pltpu.PrefetchScalarGridSpec(
            num_scalar_prefetch=1,
            grid=(owners,),
            in_specs=[pl.BlockSpec((rows, width), lambda i, ids: (0, 0))],
            out_specs=pl.BlockSpec((capacity, width), lambda i, ids: (i, 0)),
            scratch_shapes=[
                pltpu.VMEM(((rows + 2) * parts, 128), F32),
                pltpu.VMEM((capacity * parts, 128), F32),
            ],
        ),
        compiler_params=params(32),
        name="gather_rows",
    )(ids, table)


def scatter_rows(ids, counts, grads, rows, owners, capacity):
    width = grads.shape[1]
    parts = width // 128
    return pl.pallas_call(
        scatter_kernel,
        out_shape=jax.ShapeDtypeStruct((width, rows), BF),
        grid_spec=pltpu.PrefetchScalarGridSpec(
            num_scalar_prefetch=2,
            grid=(owners,),
            in_specs=[pl.BlockSpec((capacity, width), lambda i, *_: (i, 0))],
            out_specs=pl.BlockSpec((width, rows), lambda i, *_: (0, 0)),
            scratch_shapes=[
                pltpu.VMEM(((rows + 2) * parts, 128), F32),
                pltpu.VMEM(((rows + 2) * parts, 128), F32),
                pltpu.VMEM((capacity * parts, 128), F32),
            ],
        ),
        compiler_params=params(40),
        name="scatter_rows",
    )(ids, counts, grads)


def layer(arrived, slots, w_in, w_out, doc, og):
    events, width = og.shape
    wide = w_in.shape[1]
    return pl.pallas_call(
        layer_kernel,
        out_shape=(
            jax.ShapeDtypeStruct((events, width), BF),
            jax.ShapeDtypeStruct(arrived.shape, BF),
            jax.ShapeDtypeStruct((events, width), BF),
            jax.ShapeDtypeStruct((events, wide), BF),
            jax.ShapeDtypeStruct((events, width), BF),
        ),
        scratch_shapes=[
            pltpu.VMEM((events, width), BF),
            pltpu.VMEM((events, wide), BF),
            pltpu.VMEM((HEADS, events, events), BF),
            pltpu.VMEM((HEADS, events, events), BF),
            pltpu.VMEM((events, width), F32),
            pltpu.VMEM((events, width), BF),
            pltpu.VMEM((events, width), BF),
        ],
        compiler_params=params(60),
        name="layer",
    )(arrived, slots, w_in, w_out, doc, og)


def weight_grads(normed, du, gated, og):
    width = gated.shape[1]
    return pl.pallas_call(
        weights_kernel,
        out_shape=jax.ShapeDtypeStruct((width, du.shape[1] + width), BF),
        compiler_params=params(32),
        name="weight_grads",
    )(normed, du, gated, og)


def whole(table, w_in, w_out, owner, local_row, doc_ids, out_grad):
    events, lookups_each = owner.shape
    rows_owned, width = table.shape
    owners = lax.axis_size("table")
    lookups = events * lookups_each
    capacity = 2 * lookups // owners
    wide = w_in.shape[1]
    own = owner.T.reshape(lookups // 128, 128)
    loc = local_row.T.reshape(lookups // 128, 128)
    slots, requests = route(own, loc, capacity, owners, rows_owned)
    asked = lax.all_to_all(requests, "table", split_axis=0, concat_axis=0, tiled=True)
    ids = asked.reshape(owners * capacity)
    counts = jnp.sum((asked < rows_owned).astype(jnp.int32), axis=1)
    found = gather_rows(ids, table, owners, capacity).reshape(owners, capacity, width)
    arrived = lax.all_to_all(found, "table", split_axis=0, concat_axis=0, tiled=True)
    layer_out, sending, normed, du, gated = layer(
        arrived.reshape(owners * capacity, width), slots, w_in, w_out, doc_ids, out_grad
    )
    received = lax.all_to_all(
        sending.reshape(owners, capacity, width), "table", split_axis=0, concat_axis=0, tiled=True
    )
    terms = weight_grads(normed, du, gated, out_grad)
    partial = lax.psum_scatter(terms, "dp", scatter_dimension=0, tiled=True)
    partial = lax.psum(partial.astype(F32), "table").astype(BF)
    weights = lax.all_gather(partial, "dp", axis=0, tiled=True).astype(F32)
    summed = scatter_rows(
        ids, counts, received.reshape(owners * capacity, width), rows_owned, owners, capacity
    )
    mine = lax.psum_scatter(summed, "dp", scatter_dimension=0, tiled=True)
    return (layer_out, weights[:, :wide], weights[:, wide:], mine.T.astype(F32))


def solution(mesh):
    placed = (
        P("table", None),
        P(),
        P(),
        P(("dp", "table"), None),
        P(("dp", "table"), None),
        P(("dp", "table"), None),
        P(("dp", "table"), None),
    )
    return jax.shard_map(
        whole,
        mesh=mesh,
        in_specs=placed,
        out_specs=(P(("dp", "table"), None), P(), P(), P("table", "dp")),
        check_vma=False,
    )
```

time: 544 us -> 389 us (0.72)
  local copies, waits for them, and re-layouts: 103 us -> 18.4 us
  Pallas kernels: 0 us -> 74.9 us
  matrix products: 71.9 us -> 0 us
  other arithmetic: 71.9 us -> 2.46 us
    pallas_call x0 -> x5, Pallas kernels: none -> 74.9 us  [the longest x1 43.5 us: layer(): pl.pallas_call(layer_kernel, out_shape=(jax.ShapeDtypeStruct((events, wid...]
    dot_general x12 -> x0, matrix products: 71.9 us -> none  [the longest x3 25.3 us: hstu_layer(): jnp.einsum('thd,shd->hts', query_heads, key_heads, preferred_element_type...]
    reduce_scatter x0 -> x2, waiting for transfers between devices: none -> 68.4 us  [the longest x1 35.2 us: whole(): mine = lax.psum_scatter(summed, 'dp', scatter_dimension=0, tiled=True)]
    psum x1, waiting for transfers between devices: 126 us -> 86.8 us  [whole(): partial = lax.psum(partial.astype(F32), 'table').astype(BF)]
    gather x3 -> x0, local copies, waits for them, and re-layouts: 36.3 us -> none  [the longest x1 20.2 us: shards(): jnp.take(table, lax.all_to_all(requests, 'table', split_axis=0, concat_ax...]
    scatter-add x1 -> x0, other arithmetic: 32.1 us -> none  [shards(): jax.ops.segment_sum(received.reshape(owners * capacity, width).astype(jnp...]
    unnamed x3 -> x4, waiting for transfers between devices: 30.3 us -> 0.07 us
    scatter x2 -> x0, local copies, waits for them, and re-layouts: 20.9 us -> none  [the longest x1 12.8 us: shards(): sending = jnp.zeros((owners * capacity, width), jnp.bfloat16).at[slot_ind...]
  transfers between devices with their start and end apart: 3 -> 5, of which waited for: 3 -> 4; matrix products, arithmetic and copies ran while one was open for 3% -> 2% of each run, Pallas kernels for 0% -> 4%
where the time goes in v1:
time: 389 us; the launch traced here: 386 us
  waiting for transfers between devices  205 us (53%)
  Pallas kernels  74.9 us (19%)
  blocking collectives  65.9 us (17%)
  local copies, waits for them, and re-layouts  18.4 us (5%)
  between operations  13.8 us (4%)
  starting transfers between devices  5.02 us (1%)
    psum x1, waiting for transfers between devices, whole(): partial = lax.psum(partial.astype(F32), 'table').astype(BF)  86.8 us
    all_to_all x1, blocking collectives, whole(): lax.all_to_all(found, 'table', split_axis=0, concat_axis=0, tiled=True)  52.1 us
    all_to_all x1, waiting for transfers between devices, whole(): lax.all_to_all(sending.reshape(owners, capacity, width), 'table', split_a...  50.1 us
    pallas_call x1, Pallas kernels, layer(): pl.pallas_call(layer_kernel, out_shape=(jax.ShapeDtypeStruct((events, wid...  43.5 us
    reduce_scatter x1, waiting for transfers between devices, whole(): mine = lax.psum_scatter(summed, 'dp', scatter_dimension=0, tiled=True)  35.2 us
    reduce_scatter x1, waiting for transfers between devices, whole(): partial = lax.psum_scatter(terms, 'dp', scatter_dimension=0, tiled=True)  33.3 us
    pallas_call x1, Pallas kernels, scatter_rows(): pl.pallas_call(scatter_kernel, out_shape=jax.ShapeDtypeStruct((width, row...  15.8 us
    all_to_all x1, blocking collectives, whole(): lax.all_to_all(requests, 'table', split_axis=0, concat_axis=0, tiled=True)  13.8 us
  transfers between devices with their start and end apart: 5, of which 4 were waited for; matrix products, arithmetic and copies ran while one was open for 2% of the time, Pallas kernels for 4%

profile of v1, /device:TPU:1, one launch (start us, length us, event | category | flops | bytes accessed | tf_op | source)
XLA Modules:
  0.0 385.9 jit_solution(14715781682466961290)
XLA Ops:
  7.2 0.0 reduce-scatter.3.cloned.1.call-start
  7.2 1.3 reshape.35.refs_0_
  8.5 1.3 reshape.36.refs_1_
  9.8 2.1 route.1
  11.9 0.7 copy.11
  12.7 13.8 %all_to_all.19 = s32[16,1,256]{2,1,0:T(1,128)S(1)} all-to-all(s32[16,1,256]{2,1,0:T(1,128)S(1)} %copy.11), channel_id=1, replica_groups=mesh['dp'=8,'table'=16] {'table'}, dimensions={0} | all-to-all | bytes 32768 | tf_op jit(solution)/shard_map/all_to_all | solution.py:427
  26.5 2.2 copy-done.2
  28.7 9.1 %gather_rows.1 = bf16[4096,512]{1,0:T(8,128)(2,1)S(1)} custom-call(s32[4096]{0:T(1024)S(1)} %bitcast.11, bf16[4096,512]{1,0:T(8,128)(2,1)S(1)} %copy-done.2), custom_call_target="tpu_custom_call" | custom-call | tf_op jit(solution)/shard_map/gather_rows/pallas_call | solution.py:341
  37.8 52.1 %all_to_all.20 = bf16[16,256,512]{2,1,0:T(8,128)(2,1)} all-to-all(bf16[16,256,512]{2,1,0:T(8,128)(2,1)S(1)} %bitcast.10), channel_id=1, replica_groups=mesh['dp'=8,'table'=16] {'table'}, dimensions={0} | all-to-all | bytes 8388608 | tf_op jit(solution)/shard_map/all_to_all | solution.py:431
  89.9 43.5 %layer.1 = (bf16[1024,512]{1,0:T(8,128)(2,1)}, bf16[4096,512]{1,0:T(8,128)(2,1)}, bf16[1024,512]{1,0:T(8,128)(2,1)}, bf16[1024,2048]{1,0:T(8,128)(2,1)}, bf16[1024,512]{1,0:T(8,128)(2,1)}) custom-call(bf16[4096,512]{1,0:T(8,128)(2,1)} %bitcast.13, s32[16,128]{1,0:T(8,128)} %get-tuple-element.12.slot_ref, bf16[512,2048]{1,0:T(8,128)(2,1)} %w_in_ref.1, ...), custom_call_target="tpu_custom_call" | custom-call | tf_op jit(solution)/shard_map/layer/pallas_call | solution.py:384
  133.4 2.2 copy-done.3
  135.6 1.2 copy-done.4
  136.8 1.2 copy-done.5
  138.0 4.4 %weight_grads.1 = bf16[512,2560]{1,0:T(8,128)(2,1)} custom-call(bf16[1024,512]{1,0:T(8,128)(2,1)S(1)} %copy-done.4, bf16[1024,2048]{1,0:T(8,128)(2,1)S(1)} %copy-done.3, bf16[1024,512]{1,0:T(8,128)(2,1)S(1)} %copy-done.5, bf16[1024,512]{1,0:T(8,128)(2,1)S(1)} %copy-done.1), custom_call_target="tpu_custom_call" | custom-call | tf_op jit(solution)/shard_map/weight_grads/pallas_call | solution.py:409
  142.5 0.0 reduce-scatter.3.cloned.1.call-update
  142.5 0.0 all-reduce.2.cloned.1.call-start
  142.5 33.3 %reduce-scatter.3.cloned.1.call-done = bf16[64,2560]{1,0:T(8,128)(2,1)} async-done(((bf16[512,2560]{1,0:T(8,128)(2,1)}), bf16[64,2560]{1,0:T(8,128)(2,1)}) %reduce-scatter.3.cloned.1.call-update) | async-done | bytes 327696 | tf_op jit(solution)/shard_map/reduce_scatter | solution.py:439
  175.8 0.0 all-reduce.2.cloned.1.call-update
  175.8 0.0 all-gather.2.cloned.1.call-start
  175.9 86.8 %all-reduce.2.cloned.1.call-done = bf16[64,2560]{1,0:T(8,128)(2,1)} async-done(((bf16[64,2560]{1,0:T(8,128)(2,1)}), bf16[64,2560]{1,0:T(8,128)(2,1)}) %all-reduce.2.cloned.1.call-update) | async-done | bytes 327696 | tf_op jit(solution)/shard_map/psum | solution.py:440
  262.6 0.0 all-gather.2.cloned.1.call-update
  262.7 4.9 %all-to-all-start.2 = ((bf16[16,256,512]{2,1,0:T(8,128)(2,1)}), bf16[16,256,512]{2,1,0:T(8,128)(2,1)}, u32[]{:S(2)}, u32[]{:S(2)}) async-start(bf16[16,256,512]{2,1,0:T(8,128)(2,1)} %bitcast.14), calls=%async_computation.3 | async-start | bytes 8388608 | tf_op jit(solution)/shard_map/all_to_all | solution.py:435
  267.5 0.0 reduce-scatter.5.cloned.1.call-start
  267.6 0.4 fusion.cnt_ref
  268.0 50.1 %all-to-all-done.2 = bf16[16,256,512]{2,1,0:T(8,128)(2,1)} async-done(((bf16[16,256,512]{2,1,0:T(8,128)(2,1)}), bf16[16,256,512]{2,1,0:T(8,128)(2,1)}, u32[]{:S(2)}, u32[]{:S(2)}) %all-to-all-start.2) | async-done | bytes 4194336 | tf_op jit(solution)/shard_map/all_to_all | solution.py:435
  318.0 15.8 %scatter_rows.1 = bf16[512,4096]{1,0:T(8,128)(2,1)S(1)} custom-call(s32[4096]{0:T(1024)S(1)} %bitcast.12, s32[16]{0:T(128)S(1)} %fusion.cnt_ref, bf16[4096,512]{1,0:T(8,128)(2,1)} %bitcast.7.grad_ref), custom_call_target="tpu_custom_call" | custom-call | tf_op jit(solution)/shard_map/scatter_rows/pallas_call | solution.py:362
  333.8 1.9 copy-done
  335.8 0.0 all-gather.2.cloned.1.call-done
  335.8 4.1 %slice.8 = f32[512,2048]{1,0:T(8,128)} slice(bf16[512,2560]{1,0:T(8,128)(2,1)} %all-gather.2.cloned.1.call-done), slice={[0:512], [0:2048]} | slice | bytes 8388608 | tf_op jit(solution)/shard_map/slice | solution.py:446
  340.0 2.1 slice.9
  342.1 35.2 %reduce-scatter.5.cloned.1.call-done = bf16[64,4096]{1,0:T(8,128)(2,1)} async-done(((bf16[512,4096]{1,0:T(8,128)(2,1)}), bf16[64,4096]{1,0:T(8,128)(2,1)}) %reduce-scatter.5.cloned.1.call-update) | async-done | bytes 524304 | tf_op jit(solution)/shard_map/reduce_scatter | solution.py:445
  377.3 2.1 convert_bitcast_fusion
  (8 shorter events, 0.0 us)
Async XLA Ops:
  7.2 168.6 %reduce-scatter.3.cloned.1.call-start = ((), (), s32[]{:S(2)}) async-start(), calls=%async_computation.5 | async-start | bytes 2949120 | tf_op jit(solution)/shard_map/reduce_scatter | solution.py:439
  26.5 2.2 copy-start.2
  89.9 43.5 %copy-start.1 = (bf16[1024,512]{1,0:T(8,128)(2,1)S(1)}, bf16[1024,512]{1,0:T(8,128)(2,1)}, u32[]{:S(2)}) copy-start(bf16[1024,512]{1,0:T(8,128)(2,1)} %og_ref.3) | copy-start | bytes 3145732
  133.4 2.2 copy-start.3
  135.6 1.2 copy-start.4
  136.8 1.2 copy-start.5
  142.5 120.1 %all-reduce.2.cloned.1.call-start = ((), (), s32[]{:S(2)}) async-start(), calls=%async_computation.6 | async-start | bytes 655360 | tf_op jit(solution)/shard_map/psum | solution.py:440
  175.8 160.0 %all-gather.2.cloned.1.call-start = ((), (), s32[]{:S(2)}) async-start(), calls=%async_computation.7 | async-start | bytes 2949120 | tf_op jit(solution)/shard_map/all_gather | solution.py:441
  262.7 55.4 %all-to-all-start.2 = ((bf16[16,256,512]{2,1,0:T(8,128)(2,1)}), bf16[16,256,512]{2,1,0:T(8,128)(2,1)}, u32[]{:S(2)}, u32[]{:S(2)}) async-start(bf16[16,256,512]{2,1,0:T(8,128)(2,1)} %bitcast.14), calls=%async_computation.3 | async-start | bytes 8388608 | tf_op jit(solution)/shard_map/all_to_all | solution.py:435
  267.5 109.7 %reduce-scatter.5.cloned.1.call-start = ((), (), s32[]{:S(2)}) async-start(), calls=%async_computation.8 | async-start | bytes 4718592 | tf_op jit(solution)/shard_map/reduce_scatter | solution.py:445
  333.8 1.9 copy-start
Sparse Core Ops, SparseCore 0:
  142.6 33.1 reduce-scatter.2
  179.0 83.5 all-reduce.1
  264.3 27.8 all-gather.1
  335.9 41.2 reduce-scatter.4

commit v2 on v1

--- a/solution.py
+++ b/solution.py
@@ -96,30 +96,28 @@
         out_ref[:, c * 128 : (c + 1) * 128] = picked[pl.ds(c, count, stride=parts), :].astype(BF)
 
 
-def scatter_kernel(ids_ref, cnt_ref, grad_ref, out_ref, even, odd, rows_in):
+def scatter_kernel(ids_ref, cnt_ref, grad_ref, out_ref, total, rows_in):
     step = pl.program_id(0)
     count, width = grad_ref.shape
-    parts = width // 128
+    used = width // 128
     rows = out_ref.shape[1]
+    parts = rows_in.shape[0] // count
 
     @pl.when(step == 0)
     def _():
         def clear(i, carry):
-            base = pl.ds(pl.multiple_of(i * 128, 128), 128)
-            even[base, :] = jnp.zeros((128, 128), F32)
-            odd[base, :] = jnp.zeros((128, 128), F32)
+            total[pl.ds(pl.multiple_of(i * 256, 256), 256), :] = jnp.zeros((256, 128), F32)
             return carry
 
-        lax.fori_loop(0, rows * parts // 128, clear, 0)
-
-    for c in range(parts):
+        lax.fori_loop(0, rows * parts // 256, clear, 0)
+
+    for c in range(used):
         rows_in[pl.ds(c, count, stride=parts), :] = grad_ref[:, c * 128 : (c + 1) * 128].astype(F32)
 
     def add_rows(k, carry):
         for u in range(8):
             s = k * 8 + u
             row = ids_ref[step * count + s]
-            total = odd if u % 2 else even
             at = pl.ds(pl.multiple_of(row * parts, parts), parts)
             total[at, :] = (
                 total[at, :] + rows_in[pl.ds(pl.multiple_of(s * parts, parts), parts), :]
@@ -131,11 +129,10 @@
     @pl.when(step == pl.num_programs(0) - 1)
     def _():
         def flush(i, carry):
-            for c in range(parts):
-                at = pl.ds(i * (128 * parts) + c, 128, stride=parts)
-                both = even[at, :] + odd[at, :]
+            for c in range(used):
+                block = total[pl.ds(i * (128 * parts) + c, 128, stride=parts), :]
                 out_ref[c * 128 : (c + 1) * 128, pl.ds(pl.multiple_of(i * 128, 128), 128)] = (
-                    both.T.astype(BF)
+                    block.T.astype(BF)
                 )
             return carry
 
@@ -155,7 +152,24 @@
     return scale * (grad - shared - unit * along)
 
 
+def spread_columns(place_ref, width, shares):
+    column = iota((8, width), 1)
+    place = place_ref[0]
+    source = jnp.zeros((8, width), jnp.int32)
+    start = 0
+    for share in shares:
+        inside = column - 8 * start
+        piece = inside // share
+        z = (place // 2 + piece) & 3
+        core = (place + piece // 4) & 1
+        here = (z * 2 + core) * (width // 8) + start + inside - piece * share
+        source = jnp.where(inside >= 0, here, source)
+        start += share
+    return onehot(iota((width, width), 0) == source[0:1, :])
+
+
 def layer_kernel(
+    place_ref,
     arrived_ref,
     slot_ref,
     w_in_ref,
@@ -163,7 +177,8 @@
     doc_ref,
     og_ref,
     out_ref,
-    sending_ref,
+    send_a_ref,
+    send_b_ref,
     normed_ref,
     du_ref,
     gated_ref,
@@ -174,6 +189,7 @@
     mixed_ref,
     dmix_ref,
     eg_ref,
+    col_ref,
 ):
     events, width = og_ref.shape
     slots = arrived_ref.shape[0]
@@ -185,19 +201,32 @@
     slot_all = slot_ref[...]
     slot_cols = slot_all.astype(F32).T.astype(jnp.int32)
     doc_rows = doc_ref[...]
+    for r in range(lane_rows):
+        rows = slice(r * 128, (r + 1) * 128)
+        col_ref[rows, 0:1] = slot_cols[:, r : r + 1]
+        col_ref[rows, 1:2] = slot_cols[:, lane_rows + r : lane_rows + r + 1]
     doc_cols = jnp.broadcast_to(doc_rows.astype(F32), (8, events)).T[:, 0:1].astype(jnp.int32)
+    col_ref[:, 2:3] = doc_cols
     scale = head ** (-0.5)
 
-    for b in range(nblk):
-        rows = slice(b * blk, (b + 1) * blk)
-        per = blk // 128
-        first = jnp.concatenate(
-            [slot_cols[:, b * per + i : b * per + i + 1] for i in range(per)], axis=0
-        )
-        second = jnp.concatenate(
-            [slot_cols[:, lane_rows + b * per + i : lane_rows + b * per + i + 1] for i in range(per)],
-            axis=0,
-        )
+    def steps(body, total, group):
+        def several(k, carry):
+            for u in range(group):
+                body(k * group + u, carry)
+            return carry
+
+        if total == group:
+            several(0, 0)
+        else:
+            lax.fori_loop(0, total // group, several, 0)
+
+    def block_rows(b):
+        return pl.ds(pl.multiple_of(b * blk, blk), blk)
+
+    def unpack(b, carry):
+        rows = block_rows(b)
+        first = col_ref[rows, 0:1]
+        second = col_ref[rows, 1:2]
         total = jnp.zeros((blk, width), F32)
         for o in range(slots // cap_step):
             where = iota((blk, cap_step), 1) + o * cap_step
@@ -215,6 +244,9 @@
             act = u * sig
             proj_ref[rows, cols] = act.astype(BF)
             du_ref[rows, cols] = (sig + act * (1.0 - sig)).astype(BF)
+        return carry
+
+    steps(unpack, nblk, 2)
 
     def heads_forward(h, carry):
         def cols(part):
@@ -228,7 +260,7 @@
             for j in range(i + 1):
                 keys = slice(j * blk, (j + 1) * blk)
                 scores = dot(query, proj_ref[keys, cols(3)], NT) * scale
-                allowed = doc_cols[rows] == doc_rows[:, keys]
+                allowed = col_ref[rows, 2:3] == doc_rows[:, keys]
                 if i == j:
                     allowed = allowed & (iota((blk, blk), 0) >= iota((blk, blk), 1))
                 sig = 0.5 * jnp.tanh(0.5 * scores) + 0.5
@@ -243,8 +275,8 @@
 
     lax.fori_loop(0, HEADS, heads_forward, 0)
 
-    for b in range(nblk):
-        rows = slice(b * blk, (b + 1) * blk)
+    def middle(b, carry):
+        rows = block_rows(b)
         unit, spread = normal(mixed_ref[rows, :])
         gate = proj_ref[rows, 0:width].astype(F32)
         gated = (unit * gate).astype(BF)
@@ -254,6 +286,9 @@
         dmix_ref[rows, :] = normal_back(dgated * gate, unit, spread).astype(BF)
         dgate = (dgated * unit).astype(BF).astype(F32)
         du_ref[rows, 0:width] = (dgate * du_ref[rows, 0:width].astype(F32)).astype(BF)
+        return carry
+
+    steps(middle, nblk, 1)
 
     def heads_backward(h, carry):
         def cols(part):
@@ -291,14 +326,19 @@
 
     lax.fori_loop(0, HEADS, heads_backward, 0)
 
-    for b in range(nblk):
-        rows = slice(b * blk, (b + 1) * blk)
+    spread = spread_columns(place_ref, width, (send_a_ref.shape[1] // 8, send_b_ref.shape[1] // 8))
+
+    def last(b, carry):
+        rows = block_rows(b)
         dnormed = dot(du_ref[rows, :], w_in_ref[...], NT).astype(BF).astype(F32)
-        unit, spread = normal(emb_ref[rows, :].astype(F32))
-        grad = normal_back(dnormed, unit, spread) + og_ref[rows, :].astype(F32)
-        eg_ref[rows, :] = grad.astype(BF)
-
-    for o in range(slots // cap_step):
+        unit, size = normal(emb_ref[rows, :].astype(F32))
+        grad = normal_back(dnormed, unit, size) + og_ref[rows, :].astype(F32)
+        eg_ref[rows, :] = dot(grad.astype(BF), spread).astype(BF)
+        return carry
+
+    steps(last, nblk, 1)
+
+    def pack(o, carry):
         where = iota((cap_step, 128), 0) + o * cap_step
         picks = [
             onehot(
@@ -307,17 +347,35 @@
             )
             for r in range(lane_rows)
         ]
-        pick = jnp.concatenate(picks, axis=1)
-        sending_ref[o * cap_step : (o + 1) * cap_step, :] = dot(pick, eg_ref[...]).astype(BF)
-
-
-def weights_kernel(normed_ref, du_ref, gated_ref, og_ref, out_ref):
+        packed = dot(jnp.concatenate(picks, axis=1), eg_ref[...]).astype(BF)
+        at = pl.ds(pl.multiple_of(o * cap_step, cap_step), cap_step)
+        send_a_ref[at, :] = packed[:, : send_a_ref.shape[1]]
+        send_b_ref[at, :] = packed[:, send_a_ref.shape[1] :]
+        return carry
+
+    steps(pack, slots // cap_step, 16)
+
+
+def weights_kernel(place_ref, normed_ref, du_ref, gated_ref, og_ref, out_ref):
     width = gated_ref.shape[1]
     wide = du_ref.shape[1]
-    for c in range(wide // width):
-        cols = slice(c * width, (c + 1) * width)
-        out_ref[:, cols] = dot(normed_ref[...], du_ref[:, cols], TN).astype(BF)
-    out_ref[:, wide:] = dot(gated_ref[...], og_ref[...], TN).astype(BF)
+    spread = spread_columns(place_ref, width, (width // 8,))
+    normed = dot(normed_ref[...], spread).astype(BF)
+    gated = dot(gated_ref[...], spread).astype(BF)
+
+    def columns(c, carry):
+        cols = pl.ds(pl.multiple_of(c * width, width), width)
+        out_ref[:, cols] = dot(normed, du_ref[:, cols], TN).astype(BF)
+        return carry
+
+    lax.fori_loop(0, wide // width, columns, 0)
+    out_ref[:, wide:] = dot(gated, og_ref[...], TN).astype(BF)
+
+
+def finish_kernel(sum_ref, first_ref, second_ref):
+    wide = first_ref.shape[1]
+    first_ref[...] = sum_ref[:, :wide].astype(F32)
+    second_ref[...] = sum_ref[:, wide:].astype(F32)
 
 
 def params(mib, **more):
@@ -333,6 +391,25 @@
         ),
         name="route",
     )(own, loc)
+
+
+def finish(summed, wide):
+    rows, both = summed.shape
+    return pl.pallas_call(
+        finish_kernel,
+        out_shape=(
+            jax.ShapeDtypeStruct((rows, wide), F32),
+            jax.ShapeDtypeStruct((rows, both - wide), F32),
+        ),
+        grid=(8,),
+        in_specs=[pl.BlockSpec((rows // 8, both), lambda i: (i, 0))],
+        out_specs=(
+            pl.BlockSpec((rows // 8, wide), lambda i: (i, 0)),
+            pl.BlockSpec((rows // 8, both - wide), lambda i: (i, 0)),
+        ),
+        compiler_params=params(58),
+        name="finish",
+    )(summed)
 
 
 def gather_rows(ids, table, owners, capacity):
@@ -351,14 +428,14 @@
                 pltpu.VMEM((capacity * parts, 128), F32),
             ],
         ),
-        compiler_params=params(32),
+        compiler_params=params(58),
         name="gather_rows",
     )(ids, table)
 
 
 def scatter_rows(ids, counts, grads, rows, owners, capacity):
     width = grads.shape[1]
-    parts = width // 128
+    parts = 1 if width == 128 else 4
     return pl.pallas_call(
         scatter_kernel,
         out_shape=jax.ShapeDtypeStruct((width, rows), BF),
@@ -368,24 +445,28 @@
             in_specs=[pl.BlockSpec((capacity, width), lambda i, *_: (i, 0))],
             out_specs=pl.BlockSpec((width, rows), lambda i, *_: (0, 0)),
             scratch_shapes=[
-                pltpu.VMEM(((rows + 2) * parts, 128), F32),
-                pltpu.VMEM(((rows + 2) * parts, 128), F32),
+                pltpu.VMEM(((rows + 8) * parts, 128), F32),
                 pltpu.VMEM((capacity * parts, 128), F32),
             ],
         ),
-        compiler_params=params(40),
+        compiler_params=params(58),
         name="scatter_rows",
     )(ids, counts, grads)
 
 
-def layer(arrived, slots, w_in, w_out, doc, og):
+def layer(place, arrived, slots, w_in, w_out, doc, og):
     events, width = og.shape
     wide = w_in.shape[1]
+    first = (arrived.shape[0], width * 3 // 4)
+    second = (arrived.shape[0], width // 4)
+    vmem = pl.BlockSpec(memory_space=pltpu.VMEM)
     return pl.pallas_call(
         layer_kernel,
+        in_specs=[pl.BlockSpec(memory_space=pltpu.SMEM)] + [vmem] * 6,
         out_shape=(
             jax.ShapeDtypeStruct((events, width), BF),
-            jax.ShapeDtypeStruct(arrived.shape, BF),
+            jax.ShapeDtypeStruct(first, BF),
+            jax.ShapeDtypeStruct(second, BF),
             jax.ShapeDtypeStruct((events, width), BF),
             jax.ShapeDtypeStruct((events, wide), BF),
             jax.ShapeDtypeStruct((events, width), BF),
@@ -398,20 +479,56 @@
             pltpu.VMEM((events, width), F32),
             pltpu.VMEM((events, width), BF),
             pltpu.VMEM((events, width), BF),
+            pltpu.VMEM((events, 128), jnp.int32),
         ],
         compiler_params=params(60),
         name="layer",
-    )(arrived, slots, w_in, w_out, doc, og)
-
-
-def weight_grads(normed, du, gated, og):
+    )(place, arrived, slots, w_in, w_out, doc, og)
+
+
+def weight_grads(place, normed, du, gated, og):
     width = gated.shape[1]
+    vmem = pl.BlockSpec(memory_space=pltpu.VMEM)
     return pl.pallas_call(
         weights_kernel,
+        in_specs=[pl.BlockSpec(memory_space=pltpu.SMEM)] + [vmem] * 4,
         out_shape=jax.ShapeDtypeStruct((width, du.shape[1] + width), BF),
-        compiler_params=params(32),
+        compiler_params=params(58),
         name="weight_grads",
-    )(normed, du, gated, og)
+    )(place, normed, du, gated, og)
+
+
+def other_core(value):
+    return lax.ppermute(value, "dp", [(d, d ^ 1) for d in range(8)])
+
+
+def along_z(value, hop):
+    return lax.ppermute(value, "dp", [(d, ((d // 2 + hop) % 4) * 2 + d % 2) for d in range(8)])
+
+
+def ring_sum(pieces, move):
+    half = pieces.shape[1] // 2
+    far = pieces[2]
+    ahead = move(far[:half], 1)
+    behind = move(far[half:], -1)
+    up = pieces[1].astype(F32)
+    up = jnp.concatenate([up[:half] + ahead.astype(F32), up[half:]], axis=0).astype(BF)
+    down = pieces[3].astype(F32)
+    down = jnp.concatenate([down[:half], down[half:] + behind.astype(F32)], axis=0).astype(BF)
+    return pieces[0].astype(F32) + move(up, 1).astype(F32) + move(down, -1).astype(F32)
+
+
+def direct_sum(pieces, move):
+    total = pieces[0].astype(F32)
+    for hop in range(1, 4):
+        total = total + move(pieces[hop], hop).astype(F32)
+    return total
+
+
+def reduce_dp(value, along=ring_sum):
+    both = value.reshape((2, value.shape[0] // 2) + value.shape[1:])
+    mine = (both[0].astype(F32) + other_core(both[1]).astype(F32)).astype(BF)
+    return along(mine.reshape((4, mine.shape[0] // 4) + mine.shape[1:]), along_z)
 
 
 def whole(table, w_in, w_out, owner, local_row, doc_ids, out_grad):
@@ -427,23 +544,42 @@
     asked = lax.all_to_all(requests, "table", split_axis=0, concat_axis=0, tiled=True)
     ids = asked.reshape(owners * capacity)
     counts = jnp.sum((asked < rows_owned).astype(jnp.int32), axis=1)
-    found = gather_rows(ids, table, owners, capacity).reshape(owners, capacity, width)
+    found = gather_rows(ids, table, owners, capacity)
+    found = found.reshape(owners, capacity, width)
     arrived = lax.all_to_all(found, "table", split_axis=0, concat_axis=0, tiled=True)
-    layer_out, sending, normed, du, gated = layer(
-        arrived.reshape(owners * capacity, width), slots, w_in, w_out, doc_ids, out_grad
+    place = lax.axis_index("dp").astype(jnp.int32).reshape(1)
+    layer_out, send_a, send_b, normed, du, gated = layer(
+        place, arrived.reshape(owners * capacity, width), slots, w_in, w_out, doc_ids, out_grad
     )
-    received = lax.all_to_all(
-        sending.reshape(owners, capacity, width), "table", split_axis=0, concat_axis=0, tiled=True
+
+    def exchange(value):
+        return lax.all_to_all(value, "table", split_axis=0, concat_axis=0, tiled=True)
+
+    def scatter(value):
+        return scatter_rows(
+            ids, counts, value.reshape(owners * capacity, -1), rows_owned, owners, capacity
+        )
+
+    both = wide + width
+    got_a = exchange(send_a.reshape(owners, capacity, -1))
+    terms = weight_grads(place, normed, du, gated, out_grad)
+    partial = reduce_dp(terms).astype(BF)
+    lanes = width // 4
+    parts = partial.reshape(owners, -1, lanes)
+    got_b = exchange(
+        jnp.concatenate([send_b.reshape(owners, capacity, lanes), parts], axis=1)
     )
-    terms = weight_grads(normed, du, gated, out_grad)
-    partial = lax.psum_scatter(terms, "dp", scatter_dimension=0, tiled=True)
-    partial = lax.psum(partial.astype(F32), "table").astype(BF)
-    weights = lax.all_gather(partial, "dp", axis=0, tiled=True).astype(F32)
-    summed = scatter_rows(
-        ids, counts, received.reshape(owners * capacity, width), rows_owned, owners, capacity
-    )
-    mine = lax.psum_scatter(summed, "dp", scatter_dimension=0, tiled=True)
-    return (layer_out, weights[:, :wide], weights[:, wide:], mine.T.astype(F32))
+    sum_a = scatter(got_a)
+    mine = jnp.sum(got_b[:, capacity:].astype(F32), axis=0, keepdims=True).astype(BF)
+    known = exchange(jnp.broadcast_to(mine, parts.shape))
+    sum_b = scatter(got_b[:, :capacity])
+    known = known.reshape(width // 8, both)
+    gathered = lax.all_gather(known, "dp", axis=0, tiled=True)
+    grad_in, grad_out = finish(gathered, wide)
+    mine_a = reduce_dp(sum_a)
+    mine_b = reduce_dp(sum_b, direct_sum)
+    mine = jnp.concatenate([mine_a, mine_b], axis=0)
+    return (layer_out, grad_in, grad_out, mine.T)
 
 
 def solution(mesh):

time: 389 us -> 337 us (0.87)
  waiting for transfers between devices: 205 us -> 103 us
  starting transfers between devices: 5.02 us -> 44.1 us
  Pallas kernels: 74.9 us -> 110 us
  blocking collectives: 65.9 us -> 36.1 us
  other arithmetic: 2.46 us -> 11.5 us
    psum x1 -> x0, waiting for transfers between devices: 86.8 us -> none  [whole(): partial = lax.psum(partial.astype(F32), 'table').astype(BF)]
    reduce_scatter x2 -> x0, waiting for transfers between devices: 68.4 us -> none  [the longest x1 35.2 us: whole(): mine = lax.psum_scatter(summed, 'dp', scatter_dimension=0, tiled=True)]
    ppermute x0 -> x14, waiting for transfers between devices: none -> 33.5 us  [the longest x11 33.5 us: along_z(): lax.ppermute(value, 'dp', [(d, (d // 2 + hop) % 4 * 2 + d % 2) for d in r...]
    all_to_all x1, blocking collectives: 52.1 us -> 22.1 us  [exchange(): lax.all_to_all(value, 'table', split_axis=0, concat_axis=0, tiled=True)]
    ppermute x0 -> x14, starting transfers between devices: none -> 23.1 us  [the longest x11 16.8 us: along_z(): lax.ppermute(value, 'dp', [(d, (d // 2 + hop) % 4 * 2 + d % 2) for d in r...]
    all_to_all x1 -> x3, waiting for transfers between devices: 50.1 us -> 69.4 us  [the longest x1 51.8 us: whole(): lax.all_to_all(found, 'table', split_axis=0, concat_axis=0, tiled=True)]
    all_to_all x1 -> x3, starting transfers between devices: 4.86 us -> 21 us  [the longest x2 16.4 us: exchange(): lax.all_to_all(value, 'table', split_axis=0, concat_axis=0, tiled=True)]
    pallas_call x1 -> x2, Pallas kernels: 15.8 us -> 31.8 us  [scatter_rows(): pl.pallas_call(scatter_kernel, out_shape=jax.ShapeDtypeStruct((width, row...]
  transfers between devices with their start and end apart: 5 -> 18, of which waited for: 4 -> 10; matrix products, arithmetic and copies ran while one was open for 2% -> 6% of each run, Pallas kernels for 4% -> 10%
where the time goes in v2:
time: 337 us; the launch traced here: 334 us
  Pallas kernels  110 us (33%)
  waiting for transfers between devices  103 us (31%)
  starting transfers between devices  44.1 us (13%)
  blocking collectives  36.1 us (11%)
  local copies, waits for them, and re-layouts  15.1 us (4%)
  between operations  14.2 us (4%)
  other arithmetic  11.5 us (3%)
    all_to_all x1, waiting for transfers between devices, whole(): lax.all_to_all(found, 'table', split_axis=0, concat_axis=0, tiled=True)  51.8 us
    pallas_call x1, Pallas kernels, layer(): pl.pallas_call(layer_kernel, in_specs=[pl.BlockSpec(memory_space=pltpu.SM...  46.6 us
    ppermute x11, waiting for transfers between devices, along_z(): lax.ppermute(value, 'dp', [(d, (d // 2 + hop) % 4 * 2 + d % 2) for d in r...  33.5 us
    pallas_call x2, Pallas kernels, scatter_rows(): pl.pallas_call(scatter_kernel, out_shape=jax.ShapeDtypeStruct((width, row...  31.8 us
    all_to_all x1, blocking collectives, exchange(): lax.all_to_all(value, 'table', split_axis=0, concat_axis=0, tiled=True)  22.1 us
    all_to_all x2, waiting for transfers between devices, exchange(): lax.all_to_all(value, 'table', split_axis=0, concat_axis=0, tiled=True)  17.6 us
    ppermute x11, starting transfers between devices, along_z(): lax.ppermute(value, 'dp', [(d, (d // 2 + hop) % 4 * 2 + d % 2) for d in r...  16.8 us
    all_to_all x2, starting transfers between devices, exchange(): lax.all_to_all(value, 'table', split_axis=0, concat_axis=0, tiled=True)  16.4 us
  transfers between devices with their start and end apart: 18, of which 10 were waited for; matrix products, arithmetic and copies ran while one was open for 6% of the time, Pallas kernels for 10%

profile of v2, /device:TPU:1, one launch (start us, length us, event | category | flops | bytes accessed | tf_op | source)
XLA Modules:
  0.0 334.3 jit_solution(17238380337835903326)
XLA Ops:
  9.8 2.1 route.1
  12.6 13.9 %all_to_all.29 = s32[16,1,256]{2,1,0:T(1,128)} all-to-all(s32[16,1,256]{2,1,0:T(1,128)S(1)} %copy.11), channel_id=1, replica_groups=mesh['dp'=8,'table'=16] {'table'}, dimensions={0} | all-to-all | bytes 32768 | tf_op jit(solution)/shard_map/all_to_all | solution.py:544
  26.6 13.6 %gather_rows.1 = bf16[4096,512]{1,0:T(8,128)(2,1)} custom-call(s32[4096]{0:T(1024)} %bitcast.18, bf16[4096,512]{1,0:T(8,128)(2,1)} %table_ref.1), custom_call_target="tpu_custom_call" | custom-call | tf_op jit(solution)/shard_map/gather_rows/pallas_call | solution.py:418
  40.2 4.6 %all-to-all-start.1 = ((bf16[16,256,512]{2,1,0:T(8,128)(2,1)}), bf16[16,256,512]{2,1,0:T(8,128)(2,1)}, u32[]{:S(2)}, u32[]{:S(2)}) async-start(bf16[16,256,512]{2,1,0:T(8,128)(2,1)} %bitcast.13), calls=%async_computation.1 | async-start | bytes 8388608 | tf_op jit(solution)/shard_map/all_to_all | solution.py:549
  44.7 51.8 %all-to-all-done.1 = bf16[16,256,512]{2,1,0:T(8,128)(2,1)} async-done(((bf16[16,256,512]{2,1,0:T(8,128)(2,1)}), bf16[16,256,512]{2,1,0:T(8,128)(2,1)}, u32[]{:S(2)}, u32[]{:S(2)}) %all-to-all-start.1) | async-done | bytes 4194336 | tf_op jit(solution)/shard_map/all_to_all | solution.py:549
  96.5 46.6 %layer.1 = (bf16[1024,512]{1,0:T(8,128)(2,1)}, bf16[4096,384]{1,0:T(8,128)(2,1)}, bf16[4096,128]{1,0:T(8,128)(2,1)}, bf16[1024,512]{1,0:T(8,128)(2,1)}, bf16[102...) custom-call(s32[1]{0:T(128)} %bitcast.place_ref, bf16[4096,512]{1,0:T(8,128)(2,1)} %bitcast.6.arrived_ref, ...), custom_call_target="tpu_custom_call" | custom-call | tf_op jit(solution)/shard_map/layer/pallas_call | solution.py:463
  143.2 9.7 %weight_grads.1 = bf16[512,2560]{1,0:T(8,128)(2,1)} custom-call(s32[1]{0:T(128)} %bitcast.place_ref, bf16[1024,512]{1,0:T(8,128)(2,1)} %get-tuple-element.18.normed_ref, bf16[1024,2048]{1,0:T(8,128)(2,1)} %get-tuple-element.19.du_ref, bf16[1024,512]{1,0:T(8,128)(2,1)} %get-tuple-element.20.gated_ref, bf16[1024,512]{1,0:T(8,128)(2,1)} %og_ref.3), custom_call_target="tpu_custom_call" | custom-call | tf_op jit(solution)/shard_map/weight_grads/pallas_call | solution.py:492
  152.8 2.5 slice.163
  155.3 5.0 %collective-permute-start = (bf16[256,2560]{1,0:T(8,128)(2,1)}, bf16[256,2560]{1,0:T(8,128)(2,1)}, u32[]{:S(2)}, u32[]{:S(2)}) collective-permute-start(bf16[256,2560]{1,0:T(8,128)(2,1)} %slice.163), channel_id=1, source_target_pairs={{0,16},{16,0},{32,48},{48,32},{64,80},{80,64},{96,112},{112,96},{1... | collective-permute-start | bytes 3932168 | tf_op jit(solution)/shard_map/ppermute | solution.py:502
  160.2 4.8 %all-to-all-start.4 = ((bf16[16,256,384]{2,1,0:T(8,128)(2,1)}), bf16[16,256,384]{2,1,0:T(8,128)(2,1)S(1)}, u32[]{:S(2)}, u32[]{:S(2)}) async-start(bf16[16,256,384]{2,1,0:T(8,128)(2,1)} %bitcast.16), calls=%async_computation.4 | async-start | bytes 6291456 | tf_op jit(solution)/shard_map/all_to_all | solution.py:556
  165.0 2.0 add_convert_fusion.1
  168.7 2.2 collective-permute-start.3
  171.0 4.2 %collective-permute-done.1 = bf16[32,2560]{1,0:T(8,128)(2,1)S(1)} collective-permute-done((bf16[32,2560]{1,0:T(8,128)(2,1)S(1)}, bf16[32,2560]{1,0:T(8,128)(2,1)S(1)}, u32[]{:S(2)}, u32[]{:S(2)}) %collective-permute-start.1) | collective-permute-done | bytes 163872 | tf_op jit(solution)/shard_map/ppermute | solution.py:506
  175.8 2.3 collective-permute-start.4
  178.2 6.8 %collective-permute-done.2 = bf16[64,2560]{1,0:T(8,128)(2,1)S(1)} collective-permute-done((bf16[64,2560]{1,0:T(8,128)(2,1)S(1)}, bf16[64,2560]{1,0:T(8,128)(2,1)S(1)}, u32[]{:S(2)}, u32[]{:S(2)}) %collective-permute-start.2) | collective-permute-done | bytes 327712 | tf_op jit(solution)/shard_map/ppermute | solution.py:506
  186.3 2.5 pad_maximum_fusion
  188.8 17.6 %all-to-all-done.4 = bf16[16,256,384]{2,1,0:T(8,128)(2,1)S(1)} async-done(((bf16[16,256,384]{2,1,0:T(8,128)(2,1)}), bf16[16,256,384]{2,1,0:T(8,128)(2,1)S(1)}, u32[]{:S(2)}, u32[]{:S(2)}) %all-to-all-start.4) | async-done | bytes 3145760 | tf_op jit(solution)/shard_map/all_to_all | solution.py:556
  206.4 11.7 %all-to-all-start.2 = ((bf16[16,336,128]{2,1,0:T(8,128)(2,1)}), bf16[16,336,128]{2,1,0:T(8,128)(2,1)}, u32[]{:S(2)}, u32[]{:S(2)}) async-start(bf16[16,336,128]{2,1,0:T(8,128)(2,1)} %pad_maximum_fusion), calls=%async_computation.2 | async-start | bytes 2752512 | tf_op jit(solution)/shard_map/all_to_all | solution.py:556
  219.2 17.1 %scatter_rows.2 = bf16[384,4096]{1,0:T(8,128)(2,1)} custom-call(s32[4096]{0:T(1024)} %bitcast.19, s32[16]{0:T(128)} %fusion.cnt_ref, bf16[4096,384]{1,0:T(8,128)(2,1)} %bitcast.14), custom_call_target="tpu_custom_call" | custom-call | tf_op jit(solution)/shard_map/scatter_rows/pallas_call | solution.py:439
  236.2 2.7 slice.173
  239.9 2.3 slice.181
  242.2 14.7 %scatter_rows.3 = bf16[128,4096]{1,0:T(8,128)(2,1)} custom-call(s32[4096]{0:T(1024)} %bitcast.20, s32[16]{0:T(128)} %fusion.cnt_ref, bf16[4096,128]{1,0:T(8,128)(2,1)} %bitcast.15), custom_call_target="tpu_custom_call" | custom-call | tf_op jit(solution)/shard_map/scatter_rows/pallas_call | solution.py:439
  260.2 22.1 %all_to_all.30 = bf16[16,80,128]{2,1,0:T(8,128)(2,1)S(1)} all-to-all(bf16[16,80,128]{2,1,0:T(8,128)(2,1)S(1)} %broadcast_in_dim.2), channel_id=1, replica_groups=mesh['dp'=8,'table'=16] {'table'}, dimensions={0} | all-to-all | bytes 655360 | tf_op jit(solution)/shard_map/all_to_all | solution.py:556
  284.9 1.9 add_convert_fusion
  288.5 2.2 collective-permute-start.8
  290.9 2.6 collective-permute-start.12
  295.3 1.9 collective-permute-start.9
  297.8 3.9 %collective-permute-done.12 = bf16[16,4096]{1,0:T(8,128)(2,1)S(1)} collective-permute-done((bf16[16,4096]{1,0:T(8,128)(2,1)S(1)}, bf16[16,4096]{1,0:T(8,128)(2,1)S(1)}, u32[]{:S(2)}, u32[]{:S(2)}) %collective-permute-start.12) | collective-permute-done | bytes 131104 | tf_op jit(solution)/shard_map/ppermute | solution.py:506
  301.7 3.0 collective-permute-done.13
  304.8 11.6 %collective-permute-done.7 = bf16[48,4096]{1,0:T(8,128)(2,1)S(1)} collective-permute-done((bf16[48,4096]{1,0:T(8,128)(2,1)S(1)}, bf16[48,4096]{1,0:T(8,128)(2,1)S(1)}, u32[]{:S(2)}, u32[]{:S(2)}) %collective-permute-start.7) | collective-permute-done | bytes 393248 | tf_op jit(solution)/shard_map/ppermute | solution.py:506
  316.4 3.3 collective-permute-done.9
  321.2 6.3 %finish.1 = (f32[512,2048]{1,0:T(8,128)}, f32[512,512]{1,0:T(8,128)}) custom-call(bf16[512,2560]{1,0:T(8,128)(2,1)} %all-gather.2.cloned.1.call-done.sum_ref), custom_call_target="tpu_custom_call" | custom-call | tf_op jit(solution)/shard_map/finish/pallas_call | solution.py:398
  (49 shorter events, 20.5 us)
Async XLA Ops:
  40.2 56.4 %all-to-all-start.1 = ((bf16[16,256,512]{2,1,0:T(8,128)(2,1)}), bf16[16,256,512]{2,1,0:T(8,128)(2,1)}, u32[]{:S(2)}, u32[]{:S(2)}) async-start(bf16[16,256,512]{2,1,0:T(8,128)(2,1)} %bitcast.13), calls=%async_computation.1 | async-start | bytes 8388608 | tf_op jit(solution)/shard_map/all_to_all | solution.py:549
  155.3 9.7 %collective-permute-start = (bf16[256,2560]{1,0:T(8,128)(2,1)}, bf16[256,2560]{1,0:T(8,128)(2,1)}, u32[]{:S(2)}, u32[]{:S(2)}) collective-permute-start(bf16[256,2560]{1,0:T(8,128)(2,1)} %slice.163), channel_id=1, source_target_pairs={{0,16},{16,0},{32,48},{48,32},{64,80},{80,64},{96,112},{112,96},{1... | collective-permute-start | bytes 3932168 | tf_op jit(solution)/shard_map/ppermute | solution.py:502
  160.2 46.2 %all-to-all-start.4 = ((bf16[16,256,384]{2,1,0:T(8,128)(2,1)}), bf16[16,256,384]{2,1,0:T(8,128)(2,1)S(1)}, u32[]{:S(2)}, u32[]{:S(2)}) async-start(bf16[16,256,384]{2,1,0:T(8,128)(2,1)} %bitcast.16), calls=%async_computation.4 | async-start | bytes 6291456 | tf_op jit(solution)/shard_map/all_to_all | solution.py:556
  167.1 8.1 %collective-permute-start.1 = (bf16[32,2560]{1,0:T(8,128)(2,1)S(1)}, bf16[32,2560]{1,0:T(8,128)(2,1)S(1)}, u32[]{:S(2)}, u32[]{:S(2)}) collective-permute-start(bf16[32,2560]{1,0:T(8,128)(2,1)S(1)} %get-tuple-element.32), channel_id=1, source_target_pairs={{0,32},{16,48},{32,64},{48,80},{64,96},{80,112},{96,0},{112,16},{1... | collective-permute-start | bytes 491528 | tf_op jit(solution)/shard_map/ppermute | solution.py:506
  168.7 6.5 %collective-permute-start.3 = (bf16[32,2560]{1,0:T(8,128)(2,1)S(1)}, bf16[32,2560]{1,0:T(8,128)(2,1)S(1)}, u32[]{:S(2)}, u32[]{:S(2)}) collective-permute-start(bf16[32,2560]{1,0:T(8,128)(2,1)S(1)} %get-tuple-element.33), channel_id=1, source_target_pairs={{0,96},{16,112},{32,0},{48,16},{64,32},{80,48},{96,64},{112,80},{1... | collective-permute-start | bytes 491528 | tf_op jit(solution)/shard_map/ppermute | solution.py:506
  175.3 9.7 %collective-permute-start.2 = (bf16[64,2560]{1,0:T(8,128)(2,1)S(1)}, bf16[64,2560]{1,0:T(8,128)(2,1)S(1)}, u32[]{:S(2)}, u32[]{:S(2)}) collective-permute-start(bf16[64,2560]{1,0:T(8,128)(2,1)S(1)} %pad_maximum_fusion.3), channel_id=1, source_target_pairs={{0,32},{16,48},{32,64},{48,80},{64,96},{80,112},{96,0},{112,16},{1... | collective-permute-start | bytes 983048 | tf_op jit(solution)/shard_map/ppermute | solution.py:506
  175.8 9.2 %collective-permute-start.4 = (bf16[64,2560]{1,0:T(8,128)(2,1)S(1)}, bf16[64,2560]{1,0:T(8,128)(2,1)S(1)}, u32[]{:S(2)}, u32[]{:S(2)}) collective-permute-start(bf16[64,2560]{1,0:T(8,128)(2,1)S(1)} %pad_maximum_fusion.4), channel_id=1, source_target_pairs={{0,96},{16,112},{32,0},{48,16},{64,32},{80,48},{96,64},{112,80},{1... | collective-permute-start | bytes 983048 | tf_op jit(solution)/shard_map/ppermute | solution.py:506
  188.8 29.4 %copy-start.2 = (s32[16,1,256]{2,1,0:T(1,128)S(1)}, s32[16,1,256]{2,1,0:T(1,128)}, u32[]{:S(2)}) copy-start(s32[16,1,256]{2,1,0:T(1,128)} %all_to_all.29) | copy-start | bytes 49156
  206.4 12.7 %copy-start = (bf16[16,256,384]{2,1,0:T(8,128)(2,1)}, bf16[16,256,384]{2,1,0:T(8,128)(2,1)S(1)}, u32[]{:S(2)}) copy-start(bf16[16,256,384]{2,1,0:T(8,128)(2,1)S(1)} %all-to-all-done.4) | copy-start | bytes 9437188
  206.4 33.5 %all-to-all-start.2 = ((bf16[16,336,128]{2,1,0:T(8,128)(2,1)}), bf16[16,336,128]{2,1,0:T(8,128)(2,1)}, u32[]{:S(2)}, u32[]{:S(2)}) async-start(bf16[16,336,128]{2,1,0:T(8,128)(2,1)} %pad_maximum_fusion), calls=%async_computation.2 | async-start | bytes 2752512 | tf_op jit(solution)/shard_map/all_to_all | solution.py:556
  218.1 103.0 %all-gather.2.cloned.1.call-start = ((), (), s32[]{:S(2)}) async-start(), calls=%async_computation.5 | async-start | bytes 2949120 | tf_op jit(solution)/shard_map/all_gather | solution.py:577
  238.9 45.9 %collective-permute-start.5 = (bf16[192,4096]{1,0:T(8,128)(2,1)}, bf16[192,4096]{1,0:T(8,128)(2,1)}, u32[]{:S(2)}, u32[]{:S(2)}) collective-permute-start(bf16[192,4096]{1,0:T(8,128)(2,1)} %slice.173), channel_id=1, source_target_pairs={{0,16},{16,0},{32,48},{48,32},{64,80},{80,64},{96,112},{112,96},{1... | collective-permute-start | bytes 4718600 | tf_op jit(solution)/shard_map/ppermute | solution.py:502
  258.8 24.7 %collective-permute-start.10 = (bf16[64,4096]{1,0:T(8,128)(2,1)}, bf16[64,4096]{1,0:T(8,128)(2,1)}, u32[]{:S(2)}, u32[]{:S(2)}) collective-permute-start(bf16[64,4096]{1,0:T(8,128)(2,1)} %slice.183), channel_id=1, source_target_pairs={{0,16},{16,0},{32,48},{48,32},{64,80},{80,64},{96,112},{112,96},{1... | collective-permute-start | bytes 1572872 | tf_op jit(solution)/shard_map/ppermute | solution.py:502
  260.2 24.6 %copy-start.1 = (bf16[384,4096]{1,0:T(8,128)(2,1)S(1)}, bf16[384,4096]{1,0:T(8,128)(2,1)}, u32[]{:S(2)}) copy-start(bf16[384,4096]{1,0:T(8,128)(2,1)} %scatter_rows.2) | copy-start | bytes 9437188
  286.9 7.3 %collective-permute-start.6 = (bf16[24,4096]{1,0:T(8,128)(2,1)S(1)}, bf16[24,4096]{1,0:T(8,128)(2,1)S(1)}, u32[]{:S(2)}, u32[]{:S(2)}) collective-permute-start(bf16[24,4096]{1,0:T(8,128)(2,1)S(1)} %get-tuple-element.26), channel_id=1, source_target_pairs={{0,32},{16,48},{32,64},{48,80},{64,96},{80,112},{96,0},{112,16},{1... | collective-permute-start | bytes 589832 | tf_op jit(solution)/shard_map/ppermute | solution.py:506
  288.5 5.6 %collective-permute-start.8 = (bf16[24,4096]{1,0:T(8,128)(2,1)S(1)}, bf16[24,4096]{1,0:T(8,128)(2,1)S(1)}, u32[]{:S(2)}, u32[]{:S(2)}) collective-permute-start(bf16[24,4096]{1,0:T(8,128)(2,1)S(1)} %get-tuple-element.27), channel_id=1, source_target_pairs={{0,96},{16,112},{32,0},{48,16},{64,32},{80,48},{96,64},{112,80},{1... | collective-permute-start | bytes 589832 | tf_op jit(solution)/shard_map/ppermute | solution.py:506
  290.8 7.0 %collective-permute-start.11 = (bf16[16,4096]{1,0:T(8,128)(2,1)S(1)}, bf16[16,4096]{1,0:T(8,128)(2,1)S(1)}, u32[]{:S(2)}, u32[]{:S(2)}) collective-permute-start(bf16[16,4096]{1,0:T(8,128)(2,1)S(1)} %get-tuple-element.36), channel_id=1, source_target_pairs={{0,32},{16,48},{32,64},{48,80},{64,96},{80,112},{96,0},{112,16},{1... | collective-permute-start | bytes 393224 | tf_op jit(solution)/shard_map/ppermute | solution.py:506
  290.9 10.8 %collective-permute-start.12 = (bf16[16,4096]{1,0:T(8,128)(2,1)S(1)}, bf16[16,4096]{1,0:T(8,128)(2,1)S(1)}, u32[]{:S(2)}, u32[]{:S(2)}) collective-permute-start(bf16[16,4096]{1,0:T(8,128)(2,1)S(1)} %get-tuple-element.38), channel_id=1, source_target_pairs={{0,64},{16,80},{32,96},{48,112},{64,0},{80,16},{96,32},{112,48},{1... | collective-permute-start | bytes 393224 | tf_op jit(solution)/shard_map/ppermute | solution.py:506
  293.4 11.3 %collective-permute-start.13 = (bf16[16,4096]{1,0:T(8,128)(2,1)S(1)}, bf16[16,4096]{1,0:T(8,128)(2,1)S(1)}, u32[]{:S(2)}, u32[]{:S(2)}) collective-permute-start(bf16[16,4096]{1,0:T(8,128)(2,1)S(1)} %get-tuple-element.37), channel_id=1, source_target_pairs={{0,96},{16,112},{32,0},{48,16},{64,32},{80,48},{96,64},{112,80},{1... | collective-permute-start | bytes 393224 | tf_op jit(solution)/shard_map/ppermute | solution.py:506
  294.3 22.1 %collective-permute-start.7 = (bf16[48,4096]{1,0:T(8,128)(2,1)S(1)}, bf16[48,4096]{1,0:T(8,128)(2,1)S(1)}, u32[]{:S(2)}, u32[]{:S(2)}) collective-permute-start(bf16[48,4096]{1,0:T(8,128)(2,1)S(1)} %pad_maximum_fusion.1), channel_id=1, source_target_pairs={{0,32},{16,48},{32,64},{48,80},{64,96},{80,112},{96,0},{112,16},{1... | collective-permute-start | bytes 1179656 | tf_op jit(solution)/shard_map/ppermute | solution.py:506
  295.3 24.4 %collective-permute-start.9 = (bf16[48,4096]{1,0:T(8,128)(2,1)S(1)}, bf16[48,4096]{1,0:T(8,128)(2,1)S(1)}, u32[]{:S(2)}, u32[]{:S(2)}) collective-permute-start(bf16[48,4096]{1,0:T(8,128)(2,1)S(1)} %pad_maximum_fusion.2), channel_id=1, source_target_pairs={{0,96},{16,112},{32,0},{48,16},{64,32},{80,48},{96,64},{112,80},{1... | collective-permute-start | bytes 1179656 | tf_op jit(solution)/shard_map/ppermute | solution.py:506
Sparse Core Ops, SparseCore 0:
  283.6 37.4 all-gather.1

commit v3 on v2

--- a/solution.py
+++ b/solution.py
@@ -29,9 +29,22 @@
 
 
 def route_kernel(own_ref, loc_ref, slot_ref, req_ref, *, owners, capacity, dummy):
-    own = own_ref[...]
-    loc = loc_ref[...]
-    rows, lanes = own.shape
+    lanes = 128
+    rows = slot_ref.shape[0]
+
+    def stacked(ref):
+        many, events = ref.shape
+        return jnp.concatenate(
+            [
+                ref[j : j + 1, k : k + lanes]
+                for j in range(many)
+                for k in range(0, events, lanes)
+            ],
+            axis=0,
+        )
+
+    own = stacked(own_ref)
+    loc = stacked(loc_ref)
     member = jnp.concatenate([onehot(own == o) for o in range(owners)], axis=0)
     total = owners * rows
     upper = onehot(iota((lanes, lanes), 0) <= iota((lanes, lanes), 1))
@@ -96,11 +109,11 @@
         out_ref[:, c * 128 : (c + 1) * 128] = picked[pl.ds(c, count, stride=parts), :].astype(BF)
 
 
-def scatter_kernel(ids_ref, cnt_ref, grad_ref, out_ref, total, rows_in):
+def scatter_kernel(ids_ref, cnt_ref, grad_ref, keep_ref, give_ref, total, rows_in):
     step = pl.program_id(0)
     count, width = grad_ref.shape
     used = width // 128
-    rows = out_ref.shape[1]
+    half, rows = keep_ref.shape
     parts = rows_in.shape[0] // count
 
     @pl.when(step == 0)
@@ -130,10 +143,12 @@
     def _():
         def flush(i, carry):
             for c in range(used):
-                block = total[pl.ds(i * (128 * parts) + c, 128, stride=parts), :]
-                out_ref[c * 128 : (c + 1) * 128, pl.ds(pl.multiple_of(i * 128, 128), 128)] = (
-                    block.T.astype(BF)
-                )
+                block = total[pl.ds(i * (128 * parts) + c, 128, stride=parts), :].T.astype(BF)
+                at = pl.ds(pl.multiple_of(i * 128, 128), 128)
+                for q in range(2):
+                    start = c * 128 + q * 64
+                    out_ref = keep_ref if start < half else give_ref
+                    out_ref[start % half : start % half + 64, at] = block[q * 64 : (q + 1) * 64]
             return carry
 
         lax.fori_loop(0, rows // 128, flush, 0)
@@ -356,20 +371,29 @@
     steps(pack, slots // cap_step, 16)
 
 
-def weights_kernel(place_ref, normed_ref, du_ref, gated_ref, og_ref, out_ref):
+def weights_kernel(place_ref, normed_ref, du_ref, gated_ref, og_ref, keep_ref, give_ref, turned):
+    step = pl.program_id(0)
+    last = pl.num_programs(0) - 1
     width = gated_ref.shape[1]
-    wide = du_ref.shape[1]
-    spread = spread_columns(place_ref, width, (width // 8,))
-    normed = dot(normed_ref[...], spread).astype(BF)
-    gated = dot(gated_ref[...], spread).astype(BF)
-
-    def columns(c, carry):
-        cols = pl.ds(pl.multiple_of(c * width, width), width)
-        out_ref[:, cols] = dot(normed, du_ref[:, cols], TN).astype(BF)
-        return carry
-
-    lax.fori_loop(0, wide // width, columns, 0)
-    out_ref[:, wide:] = dot(gated, og_ref[...], TN).astype(BF)
+    half = width // 2
+
+    @pl.when(step == 0)
+    def _():
+        spread = spread_columns(place_ref, width, (width // 8,))
+        turned[0] = dot(normed_ref[...], spread).astype(BF)
+        turned[1] = dot(gated_ref[...], spread).astype(BF)
+
+    def put(value):
+        keep_ref[...] = value[:half].astype(BF)
+        give_ref[...] = value[half:].astype(BF)
+
+    @pl.when(step < last)
+    def _():
+        put(dot(turned[0], du_ref[...], TN))
+
+    @pl.when(step == last)
+    def _():
+        put(dot(turned[1], og_ref[...], TN))
 
 
 def finish_kernel(sum_ref, first_ref, second_ref):
@@ -386,7 +410,7 @@
     return pl.pallas_call(
         lambda *refs: route_kernel(*refs, owners=owners, capacity=capacity, dummy=dummy),
         out_shape=(
-            jax.ShapeDtypeStruct(own.shape, jnp.int32),
+            jax.ShapeDtypeStruct((own.size // 128, 128), jnp.int32),
             jax.ShapeDtypeStruct((owners, capacity), jnp.int32),
         ),
         name="route",
@@ -407,7 +431,7 @@
             pl.BlockSpec((rows // 8, wide), lambda i: (i, 0)),
             pl.BlockSpec((rows // 8, both - wide), lambda i: (i, 0)),
         ),
-        compiler_params=params(58),
+        compiler_params=params(16),
         name="finish",
     )(summed)
 
@@ -428,28 +452,28 @@
                 pltpu.VMEM((capacity * parts, 128), F32),
             ],
         ),
-        compiler_params=params(58),
+        compiler_params=params(32),
         name="gather_rows",
     )(ids, table)
 
 
 def scatter_rows(ids, counts, grads, rows, owners, capacity):
-    width = grads.shape[1]
+    width = grads.shape[2]
     parts = 1 if width == 128 else 4
     return pl.pallas_call(
         scatter_kernel,
-        out_shape=jax.ShapeDtypeStruct((width, rows), BF),
+        out_shape=(jax.ShapeDtypeStruct((width // 2, rows), BF),) * 2,
         grid_spec=pltpu.PrefetchScalarGridSpec(
             num_scalar_prefetch=2,
             grid=(owners,),
-            in_specs=[pl.BlockSpec((capacity, width), lambda i, *_: (i, 0))],
-            out_specs=pl.BlockSpec((width, rows), lambda i, *_: (0, 0)),
+            in_specs=[pl.BlockSpec((None, capacity, width), lambda i, *_: (i, 0, 0))],
+            out_specs=(pl.BlockSpec((width // 2, rows), lambda i, *_: (0, 0)),) * 2,
             scratch_shapes=[
                 pltpu.VMEM(((rows + 8) * parts, 128), F32),
                 pltpu.VMEM((capacity * parts, 128), F32),
             ],
         ),
-        compiler_params=params(58),
+        compiler_params=params(40),
         name="scatter_rows",
     )(ids, counts, grads)
 
@@ -487,12 +511,23 @@
 
 
 def weight_grads(place, normed, du, gated, og):
-    width = gated.shape[1]
-    vmem = pl.BlockSpec(memory_space=pltpu.VMEM)
+    events, width = gated.shape
+    steps = du.shape[1] // width
+    whole = pl.BlockSpec((events, width), lambda c: (0, 0))
+    part = pl.BlockSpec((width // 2, width), lambda c: (0, c))
     return pl.pallas_call(
         weights_kernel,
-        in_specs=[pl.BlockSpec(memory_space=pltpu.SMEM)] + [vmem] * 4,
-        out_shape=jax.ShapeDtypeStruct((width, du.shape[1] + width), BF),
+        grid=(steps + 1,),
+        in_specs=[
+            pl.BlockSpec(memory_space=pltpu.SMEM),
+            whole,
+            pl.BlockSpec((events, width), lambda c: (0, jnp.minimum(c, steps - 1))),
+            whole,
+            whole,
+        ],
+        out_specs=(part, part),
+        out_shape=(jax.ShapeDtypeStruct((width // 2, du.shape[1] + width), BF),) * 2,
+        scratch_shapes=[pltpu.VMEM((2, events, width), BF)],
         compiler_params=params(58),
         name="weight_grads",
     )(place, normed, du, gated, og)
@@ -520,14 +555,15 @@
 
 def direct_sum(pieces, move):
     total = pieces[0].astype(F32)
-    for hop in range(1, 4):
-        total = total + move(pieces[hop], hop).astype(F32)
+    moved = [move(pieces[hop], hop) for hop in range(1, 4)]
+    for value in moved:
+        total = total + value.astype(F32)
     return total
 
 
 def reduce_dp(value, along=ring_sum):
-    both = value.reshape((2, value.shape[0] // 2) + value.shape[1:])
-    mine = (both[0].astype(F32) + other_core(both[1]).astype(F32)).astype(BF)
+    keep, give = value
+    mine = (keep.astype(F32) + other_core(give).astype(F32)).astype(BF)
     return along(mine.reshape((4, mine.shape[0] // 4) + mine.shape[1:]), along_z)
 
 
@@ -538,9 +574,7 @@
     lookups = events * lookups_each
     capacity = 2 * lookups // owners
     wide = w_in.shape[1]
-    own = owner.T.reshape(lookups // 128, 128)
-    loc = local_row.T.reshape(lookups // 128, 128)
-    slots, requests = route(own, loc, capacity, owners, rows_owned)
+    slots, requests = route(owner.T, local_row.T, capacity, owners, rows_owned)
     asked = lax.all_to_all(requests, "table", split_axis=0, concat_axis=0, tiled=True)
     ids = asked.reshape(owners * capacity)
     counts = jnp.sum((asked < rows_owned).astype(jnp.int32), axis=1)
@@ -556,9 +590,7 @@
         return lax.all_to_all(value, "table", split_axis=0, concat_axis=0, tiled=True)
 
     def scatter(value):
-        return scatter_rows(
-            ids, counts, value.reshape(owners * capacity, -1), rows_owned, owners, capacity
-        )
+        return scatter_rows(ids, counts, value, rows_owned, owners, capacity)
 
     both = wide + width
     got_a = exchange(send_a.reshape(owners, capacity, -1))
@@ -572,7 +604,7 @@
     sum_a = scatter(got_a)
     mine = jnp.sum(got_b[:, capacity:].astype(F32), axis=0, keepdims=True).astype(BF)
     known = exchange(jnp.broadcast_to(mine, parts.shape))
-    sum_b = scatter(got_b[:, :capacity])
+    sum_b = scatter(got_b)
     known = known.reshape(width // 8, both)
     gathered = lax.all_gather(known, "dp", axis=0, tiled=True)
     grad_in, grad_out = finish(gathered, wide)

time: 337 us -> 319 us (0.947)
  Pallas kernels: 110 us -> 95.1 us
  waiting for transfers between devices: 103 us -> 109 us
  local copies, waits for them, and re-layouts: 15.1 us -> 10.3 us
    slice x5 -> x1, local copies, waits for them, and re-layouts: 9.35 us -> 0.03 us  [direct_sum(): moved = [move(pieces[hop], hop) for hop in range(1, 4)]]
    pallas_call x3, Pallas kernels: 41.5 us -> 33.7 us  [the longest x2 24.8 us: scatter_rows(): pl.pallas_call(scatter_kernel, out_shape=(jax.ShapeDtypeStruct((width //...]
    unnamed x6 -> x10, local copies, waits for them, and re-layouts: 0.01 us -> 7.1 us
    all_to_all x2, waiting for transfers between devices: 17.6 us -> 23 us  [exchange(): lax.all_to_all(value, 'table', split_axis=0, concat_axis=0, tiled=True)]
    pallas_call x1, Pallas kernels: 13.6 us -> 9.06 us  [gather_rows(): pl.pallas_call(gather_kernel, out_shape=jax.ShapeDtypeStruct((owners * ca...]
  transfers between devices with their start and end apart: 18 -> 18, of which waited for: 10 -> 11; matrix products, arithmetic and copies ran while one was open for 6% -> 4% of each run, Pallas kernels for 10% -> 8%
where the time goes in v3:
time: 319 us; the launch traced here: 318 us
  waiting for transfers between devices  109 us (34%)
  Pallas kernels  95.1 us (30%)
  starting transfers between devices  47 us (15%)
  blocking collectives  32.8 us (10%)
  between operations  14.2 us (4%)
  local copies, waits for them, and re-layouts  10.3 us (3%)
  other arithmetic  9.67 us (3%)
    all_to_all x1, waiting for transfers between devices, whole(): lax.all_to_all(found, 'table', split_axis=0, concat_axis=0, tiled=True)  51.8 us
    pallas_call x1, Pallas kernels, layer(): pl.pallas_call(layer_kernel, in_specs=[pl.BlockSpec(memory_space=pltpu.SM...  46.6 us
    ppermute x11, waiting for transfers between devices, along_z(): lax.ppermute(value, 'dp', [(d, (d // 2 + hop) % 4 * 2 + d % 2) for d in r...  33 us
    pallas_call x2, Pallas kernels, scatter_rows(): pl.pallas_call(scatter_kernel, out_shape=(jax.ShapeDtypeStruct((width //...  24.8 us
    all_to_all x2, waiting for transfers between devices, exchange(): lax.all_to_all(value, 'table', split_axis=0, concat_axis=0, tiled=True)  23 us
    all_to_all x1, blocking collectives, exchange(): lax.all_to_all(value, 'table', split_axis=0, concat_axis=0, tiled=True)  19 us
    ppermute x11, starting transfers between devices, along_z(): lax.ppermute(value, 'dp', [(d, (d // 2 + hop) % 4 * 2 + d % 2) for d in r...  16.8 us
    all_to_all x2, starting transfers between devices, exchange(): lax.all_to_all(value, 'table', split_axis=0, concat_axis=0, tiled=True)  16.4 us
  transfers between devices with their start and end apart: 18, of which 11 were waited for; matrix products, arithmetic and copies ran while one was open for 4% of the time, Pallas kernels for 8%

profile of v3, /device:TPU:1, one launch (start us, length us, event | category | flops | bytes accessed | tf_op | source)
XLA Modules:
  0.0 318.1 jit_solution(5762725997000066752)
XLA Ops:
  7.2 2.1 route.1
  10.0 13.8 %all_to_all.29 = s32[16,1,256]{2,1,0:T(1,128)S(1)} all-to-all(s32[16,1,256]{2,1,0:T(1,128)S(1)} %copy.11), channel_id=1, replica_groups=mesh['dp'=8,'table'=16] {'table'}, dimensions={0} | all-to-all | bytes 32768 | tf_op jit(solution)/shard_map/all_to_all | solution.py:578
  23.8 2.2 copy-done.1
  26.0 9.1 %gather_rows.1 = bf16[4096,512]{1,0:T(8,128)(2,1)S(1)} custom-call(s32[4096]{0:T(1024)S(1)} %bitcast.12, bf16[4096,512]{1,0:T(8,128)(2,1)S(1)} %copy-done.1), custom_call_target="tpu_custom_call" | custom-call | tf_op jit(solution)/shard_map/gather_rows/pallas_call | solution.py:442
  35.1 2.0 copy-done
  37.1 4.5 %all-to-all-start.1 = ((bf16[16,256,512]{2,1,0:T(8,128)(2,1)}), bf16[16,256,512]{2,1,0:T(8,128)(2,1)}, u32[]{:S(2)}, u32[]{:S(2)}) async-start(bf16[16,256,512]{2,1,0:T(8,128)(2,1)} %bitcast.11), calls=%async_computation.1 | async-start | bytes 8388608 | tf_op jit(solution)/shard_map/all_to_all | solution.py:583
  41.7 51.8 %all-to-all-done.1 = bf16[16,256,512]{2,1,0:T(8,128)(2,1)} async-done(((bf16[16,256,512]{2,1,0:T(8,128)(2,1)}), bf16[16,256,512]{2,1,0:T(8,128)(2,1)}, u32[]{:S(2)}, u32[]{:S(2)}) %all-to-all-start.1) | async-done | bytes 4194336 | tf_op jit(solution)/shard_map/all_to_all | solution.py:583
  93.5 46.6 %layer.1 = (bf16[1024,512]{1,0:T(8,128)(2,1)}, bf16[4096,384]{1,0:T(8,128)(2,1)}, bf16[4096,128]{1,0:T(8,128)(2,1)}, bf16[1024,512]{1,0:T(8,128)(2,1)}, bf16[102...) custom-call(s32[1]{0:T(128)} %bitcast.place_ref, bf16[4096,512]{1,0:T(8,128)(2,1)} %bitcast.6.arrived_ref, ...), custom_call_target="tpu_custom_call" | custom-call | tf_op jit(solution)/shard_map/layer/pallas_call | solution.py:487
  140.1 8.9 %weight_grads.1 = (bf16[256,2560]{1,0:T(8,128)(2,1)}, bf16[256,2560]{1,0:T(8,128)(2,1)}) custom-call(s32[1]{0:T(128)} %bitcast.place_ref, bf16[1024,512]{1,0:T(8,128)(2,1)} %get-tuple-element.24.normed_ref, bf16[1024,2048]{1,0:T(8,128)(2,1)} %get-tuple-element.25.du_ref, bf16[1024,512]{1,0:T(8,128)(2,1)} %get-tuple-element.26.gated_ref, bf16[1024,512]{1,0:T(8,128)(2,1)} %og_ref.3), custom_call_target="tpu_custom_call" | custom-call | tf_op jit(solution)/shard_map/weight_grads/pallas_call | solution.py:518
  148.9 5.0 %collective-permute-start = (bf16[256,2560]{1,0:T(8,128)(2,1)}, bf16[256,2560]{1,0:T(8,128)(2,1)}, u32[]{:S(2)}, u32[]{:S(2)}) collective-permute-start(bf16[256,2560]{1,0:T(8,128)(2,1)} %get-tuple-element.28), channel_id=1, source_target_pairs={{0,16},{16,0},{32,48},{48,32},{64,80},{80,64},{96,112},{112,96},{1... | collective-permute-start | bytes 3932168 | tf_op jit(solution)/shard_map/ppermute | solution.py:537
  153.9 4.7 %all-to-all-start.4 = ((bf16[16,256,384]{2,1,0:T(8,128)(2,1)}), bf16[16,256,384]{2,1,0:T(8,128)(2,1)S(1)}, u32[]{:S(2)}, u32[]{:S(2)}) async-start(bf16[16,256,384]{2,1,0:T(8,128)(2,1)} %bitcast.15), calls=%async_computation.4 | async-start | bytes 6291456 | tf_op jit(solution)/shard_map/all_to_all | solution.py:590
  158.6 2.0 add_convert_fusion.1
  162.4 2.2 collective-permute-start.3
  164.6 4.2 %collective-permute-done.1 = bf16[32,2560]{1,0:T(8,128)(2,1)S(1)} collective-permute-done((bf16[32,2560]{1,0:T(8,128)(2,1)S(1)}, bf16[32,2560]{1,0:T(8,128)(2,1)S(1)}, u32[]{:S(2)}, u32[]{:S(2)}) %collective-permute-start.1) | collective-permute-done | bytes 163872 | tf_op jit(solution)/shard_map/ppermute | solution.py:541
  169.5 2.3 collective-permute-start.4
  171.8 6.8 %collective-permute-done.2 = bf16[64,2560]{1,0:T(8,128)(2,1)S(1)} collective-permute-done((bf16[64,2560]{1,0:T(8,128)(2,1)S(1)}, bf16[64,2560]{1,0:T(8,128)(2,1)S(1)}, u32[]{:S(2)}, u32[]{:S(2)}) %collective-permute-start.2) | collective-permute-done | bytes 327712 | tf_op jit(solution)/shard_map/ppermute | solution.py:541
  179.9 2.5 pad_maximum_fusion
  182.5 17.6 %all-to-all-done.4.grad_ref = bf16[16,256,384]{2,1,0:T(8,128)(2,1)S(1)} async-done(((bf16[16,256,384]{2,1,0:T(8,128)(2,1)}), bf16[16,256,384]{2,1,0:T(8,128)(2,1)S(1)}, u32[]{:S(2)}, u32[]{:S(2)}) %all-to-all-start.4) | async-done | bytes 3145760 | tf_op jit(solution)/shard_map/all_to_all | solution.py:590
  200.1 11.7 %all-to-all-start.2 = ((bf16[16,336,128]{2,1,0:T(8,128)(2,1)}), bf16[16,336,128]{2,1,0:T(8,128)(2,1)}, u32[]{:S(2)}, u32[]{:S(2)}) async-start(bf16[16,336,128]{2,1,0:T(8,128)(2,1)} %pad_maximum_fusion), calls=%async_computation.2 | async-start | bytes 2752512 | tf_op jit(solution)/shard_map/all_to_all | solution.py:590
  212.2 10.9 %scatter_rows.2 = (bf16[192,4096]{1,0:T(8,128)(2,1)S(1)}, bf16[192,4096]{1,0:T(8,128)(2,1)}) custom-call(s32[4096]{0:T(1024)S(1)} %bitcast.13, s32[16]{0:T(128)S(1)} %fusion.cnt_ref, bf16[16,256,384]{2,1,0:T(8,128)(2,1)S(1)} %all-to-all-done.4.grad_ref), custom_call_target="tpu_custom_call" | custom-call | tf_op jit(solution)/shard_map/scatter_rows/pallas_call | solution.py:463
  225.2 5.4 %all-to-all-done.2.grad_ref = bf16[16,336,128]{2,1,0:T(8,128)(2,1)} async-done(((bf16[16,336,128]{2,1,0:T(8,128)(2,1)}), bf16[16,336,128]{2,1,0:T(8,128)(2,1)}, u32[]{:S(2)}, u32[]{:S(2)}) %all-to-all-start.2) | async-done | bytes 1376288 | tf_op jit(solution)/shard_map/all_to_all | solution.py:590
  230.6 13.9 %scatter_rows.3 = (bf16[64,4096]{1,0:T(8,128)(2,1)S(1)}, bf16[64,4096]{1,0:T(8,128)(2,1)S(1)}) custom-call(s32[4096]{0:T(1024)S(1)} %bitcast.14, s32[16]{0:T(128)S(1)} %fusion.cnt_ref, bf16[16,336,128]{2,1,0:T(8,128)(2,1)} %all-to-all-done.2.grad_ref), custom_call_target="tpu_custom_call" | custom-call | tf_op jit(solution)/shard_map/scatter_rows/pallas_call | solution.py:463
  244.6 3.3 %collective-permute-start.10 = (bf16[64,4096]{1,0:T(8,128)(2,1)S(1)}, bf16[64,4096]{1,0:T(8,128)(2,1)S(1)}, u32[]{:S(2)}, u32[]{:S(2)}) collective-permute-start(bf16[64,4096]{1,0:T(8,128)(2,1)S(1)} %get-tuple-element.35), channel_id=1, source_target_pairs={{0,16},{16,0},{32,48},{48,32},{64,80},{80,64},{96,112},{112,96},{1... | collective-permute-start | bytes 1572872 | tf_op jit(solution)/shard_map/ppermute | solution.py:537
  249.0 19.0 %all_to_all.30 = bf16[16,80,128]{2,1,0:T(8,128)(2,1)S(1)} all-to-all(bf16[16,80,128]{2,1,0:T(8,128)(2,1)S(1)} %broadcast_in_dim.2), channel_id=1, replica_groups=mesh['dp'=8,'table'=16] {'table'}, dimensions={0} | all-to-all | bytes 655360 | tf_op jit(solution)/shard_map/all_to_all | solution.py:590
  269.2 1.9 add_convert_fusion
  273.0 2.2 collective-permute-start.8
  275.3 2.6 collective-permute-start.12
  279.6 1.9 collective-permute-start.9
  282.2 2.7 collective-permute-done.12
  286.7 13.7 %collective-permute-done.7 = bf16[48,4096]{1,0:T(8,128)(2,1)S(1)} collective-permute-done((bf16[48,4096]{1,0:T(8,128)(2,1)S(1)}, bf16[48,4096]{1,0:T(8,128)(2,1)S(1)}, u32[]{:S(2)}, u32[]{:S(2)}) %collective-permute-start.7) | collective-permute-done | bytes 393248 | tf_op jit(solution)/shard_map/ppermute | solution.py:541
  300.3 3.2 %collective-permute-done.9 = bf16[48,4096]{1,0:T(8,128)(2,1)S(1)} collective-permute-done((bf16[48,4096]{1,0:T(8,128)(2,1)S(1)}, bf16[48,4096]{1,0:T(8,128)(2,1)S(1)}, u32[]{:S(2)}, u32[]{:S(2)}) %collective-permute-start.9) | collective-permute-done | bytes 393248 | tf_op jit(solution)/shard_map/ppermute | solution.py:541
  307.6 3.7 %finish.1 = (f32[512,2048]{1,0:T(8,128)}, f32[512,512]{1,0:T(8,128)}) custom-call(bf16[512,2560]{1,0:T(8,128)(2,1)S(1)} %copy-done.2), custom_call_target="tpu_custom_call" | custom-call | tf_op jit(solution)/shard_map/finish/pallas_call | solution.py:422
  (47 shorter events, 19.5 us)
Async XLA Ops:
  23.8 2.2 copy-start.1
  35.1 2.0 copy-start
  37.1 56.3 %all-to-all-start.1 = ((bf16[16,256,512]{2,1,0:T(8,128)(2,1)}), bf16[16,256,512]{2,1,0:T(8,128)(2,1)}, u32[]{:S(2)}, u32[]{:S(2)}) async-start(bf16[16,256,512]{2,1,0:T(8,128)(2,1)} %bitcast.11), calls=%async_computation.1 | async-start | bytes 8388608 | tf_op jit(solution)/shard_map/all_to_all | solution.py:583
  148.9 9.7 %collective-permute-start = (bf16[256,2560]{1,0:T(8,128)(2,1)}, bf16[256,2560]{1,0:T(8,128)(2,1)}, u32[]{:S(2)}, u32[]{:S(2)}) collective-permute-start(bf16[256,2560]{1,0:T(8,128)(2,1)} %get-tuple-element.28), channel_id=1, source_target_pairs={{0,16},{16,0},{32,48},{48,32},{64,80},{80,64},{96,112},{112,96},{1... | collective-permute-start | bytes 3932168 | tf_op jit(solution)/shard_map/ppermute | solution.py:537
  153.9 46.2 %all-to-all-start.4 = ((bf16[16,256,384]{2,1,0:T(8,128)(2,1)}), bf16[16,256,384]{2,1,0:T(8,128)(2,1)S(1)}, u32[]{:S(2)}, u32[]{:S(2)}) async-start(bf16[16,256,384]{2,1,0:T(8,128)(2,1)} %bitcast.15), calls=%async_computation.4 | async-start | bytes 6291456 | tf_op jit(solution)/shard_map/all_to_all | solution.py:590
  160.7 8.1 %collective-permute-start.1 = (bf16[32,2560]{1,0:T(8,128)(2,1)S(1)}, bf16[32,2560]{1,0:T(8,128)(2,1)S(1)}, u32[]{:S(2)}, u32[]{:S(2)}) collective-permute-start(bf16[32,2560]{1,0:T(8,128)(2,1)S(1)} %get-tuple-element.44), channel_id=1, source_target_pairs={{0,32},{16,48},{32,64},{48,80},{64,96},{80,112},{96,0},{112,16},{1... | collective-permute-start | bytes 491528 | tf_op jit(solution)/shard_map/ppermute | solution.py:541
  162.4 6.4 %collective-permute-start.3 = (bf16[32,2560]{1,0:T(8,128)(2,1)S(1)}, bf16[32,2560]{1,0:T(8,128)(2,1)S(1)}, u32[]{:S(2)}, u32[]{:S(2)}) collective-permute-start(bf16[32,2560]{1,0:T(8,128)(2,1)S(1)} %get-tuple-element.45), channel_id=1, source_target_pairs={{0,96},{16,112},{32,0},{48,16},{64,32},{80,48},{96,64},{112,80},{1... | collective-permute-start | bytes 491528 | tf_op jit(solution)/shard_map/ppermute | solution.py:541
  169.0 9.7 %collective-permute-start.2 = (bf16[64,2560]{1,0:T(8,128)(2,1)S(1)}, bf16[64,2560]{1,0:T(8,128)(2,1)S(1)}, u32[]{:S(2)}, u32[]{:S(2)}) collective-permute-start(bf16[64,2560]{1,0:T(8,128)(2,1)S(1)} %pad_maximum_fusion.3), channel_id=1, source_target_pairs={{0,32},{16,48},{32,64},{48,80},{64,96},{80,112},{96,0},{112,16},{1... | collective-permute-start | bytes 983048 | tf_op jit(solution)/shard_map/ppermute | solution.py:541
  169.5 9.2 %collective-permute-start.4 = (bf16[64,2560]{1,0:T(8,128)(2,1)S(1)}, bf16[64,2560]{1,0:T(8,128)(2,1)S(1)}, u32[]{:S(2)}, u32[]{:S(2)}) collective-permute-start(bf16[64,2560]{1,0:T(8,128)(2,1)S(1)} %pad_maximum_fusion.4), channel_id=1, source_target_pairs={{0,96},{16,112},{32,0},{48,16},{64,32},{80,48},{96,64},{112,80},{1... | collective-permute-start | bytes 983048 | tf_op jit(solution)/shard_map/ppermute | solution.py:541
  200.1 30.6 %all-to-all-start.2 = ((bf16[16,336,128]{2,1,0:T(8,128)(2,1)}), bf16[16,336,128]{2,1,0:T(8,128)(2,1)}, u32[]{:S(2)}, u32[]{:S(2)}) async-start(bf16[16,336,128]{2,1,0:T(8,128)(2,1)} %pad_maximum_fusion), calls=%async_computation.2 | async-start | bytes 2752512 | tf_op jit(solution)/shard_map/all_to_all | solution.py:590
  211.7 94.1 %all-gather.2.cloned.1.call-start = ((), (), s32[]{:S(2)}) async-start(), calls=%async_computation.5 | async-start | bytes 2949120 | tf_op jit(solution)/shard_map/all_gather | solution.py:609
  223.1 1.2 copy-start.3
  224.2 45.0 %collective-permute-start.5 = (bf16[192,4096]{1,0:T(8,128)(2,1)}, bf16[192,4096]{1,0:T(8,128)(2,1)}, u32[]{:S(2)}, u32[]{:S(2)}) collective-permute-start(bf16[192,4096]{1,0:T(8,128)(2,1)} %get-tuple-element.33), channel_id=1, source_target_pairs={{0,16},{16,0},{32,48},{48,32},{64,80},{80,64},{96,112},{112,96},{1... | collective-permute-start | bytes 4718600 | tf_op jit(solution)/shard_map/ppermute | solution.py:537
  244.6 24.5 %collective-permute-start.10 = (bf16[64,4096]{1,0:T(8,128)(2,1)S(1)}, bf16[64,4096]{1,0:T(8,128)(2,1)S(1)}, u32[]{:S(2)}, u32[]{:S(2)}) collective-permute-start(bf16[64,4096]{1,0:T(8,128)(2,1)S(1)} %get-tuple-element.35), channel_id=1, source_target_pairs={{0,16},{16,0},{32,48},{48,32},{64,80},{80,64},{96,112},{112,96},{1... | collective-permute-start | bytes 1572872 | tf_op jit(solution)/shard_map/ppermute | solution.py:537
  249.0 20.3 %copy-start.4 = (bf16[192,4096]{1,0:T(8,128)(2,1)S(1)}, bf16[192,4096]{1,0:T(8,128)(2,1)}, u32[]{:S(2)}) copy-start(bf16[192,4096]{1,0:T(8,128)(2,1)} %copy-done.3) | copy-start | bytes 4718596
  271.2 7.3 %collective-permute-start.6 = (bf16[24,4096]{1,0:T(8,128)(2,1)S(1)}, bf16[24,4096]{1,0:T(8,128)(2,1)S(1)}, u32[]{:S(2)}, u32[]{:S(2)}) collective-permute-start(bf16[24,4096]{1,0:T(8,128)(2,1)S(1)} %get-tuple-element.38), channel_id=1, source_target_pairs={{0,32},{16,48},{32,64},{48,80},{64,96},{80,112},{96,0},{112,16},{1... | collective-permute-start | bytes 589832 | tf_op jit(solution)/shard_map/ppermute | solution.py:541
  273.0 5.6 %collective-permute-start.8 = (bf16[24,4096]{1,0:T(8,128)(2,1)S(1)}, bf16[24,4096]{1,0:T(8,128)(2,1)S(1)}, u32[]{:S(2)}, u32[]{:S(2)}) collective-permute-start(bf16[24,4096]{1,0:T(8,128)(2,1)S(1)} %get-tuple-element.39), channel_id=1, source_target_pairs={{0,96},{16,112},{32,0},{48,16},{64,32},{80,48},{96,64},{112,80},{1... | collective-permute-start | bytes 589832 | tf_op jit(solution)/shard_map/ppermute | solution.py:541
  275.2 7.0 %collective-permute-start.11 = (bf16[16,4096]{1,0:T(8,128)(2,1)S(1)}, bf16[16,4096]{1,0:T(8,128)(2,1)S(1)}, u32[]{:S(2)}, u32[]{:S(2)}) collective-permute-start(bf16[16,4096]{1,0:T(8,128)(2,1)S(1)} %get-tuple-element.48), channel_id=1, source_target_pairs={{0,32},{16,48},{32,64},{48,80},{64,96},{80,112},{96,0},{112,16},{1... | collective-permute-start | bytes 393224 | tf_op jit(solution)/shard_map/ppermute | solution.py:541
  275.3 9.7 %collective-permute-start.12 = (bf16[16,4096]{1,0:T(8,128)(2,1)S(1)}, bf16[16,4096]{1,0:T(8,128)(2,1)S(1)}, u32[]{:S(2)}, u32[]{:S(2)}) collective-permute-start(bf16[16,4096]{1,0:T(8,128)(2,1)S(1)} %get-tuple-element.50), channel_id=1, source_target_pairs={{0,64},{16,80},{32,96},{48,112},{64,0},{80,16},{96,32},{112,48},{1... | collective-permute-start | bytes 393224 | tf_op jit(solution)/shard_map/ppermute | solution.py:541
  277.8 8.8 %collective-permute-start.13 = (bf16[16,4096]{1,0:T(8,128)(2,1)S(1)}, bf16[16,4096]{1,0:T(8,128)(2,1)S(1)}, u32[]{:S(2)}, u32[]{:S(2)}) collective-permute-start(bf16[16,4096]{1,0:T(8,128)(2,1)S(1)} %get-tuple-element.49), channel_id=1, source_target_pairs={{0,96},{16,112},{32,0},{48,16},{64,32},{80,48},{96,64},{112,80},{1... | collective-permute-start | bytes 393224 | tf_op jit(solution)/shard_map/ppermute | solution.py:541
  278.7 21.6 %collective-permute-start.7 = (bf16[48,4096]{1,0:T(8,128)(2,1)S(1)}, bf16[48,4096]{1,0:T(8,128)(2,1)S(1)}, u32[]{:S(2)}, u32[]{:S(2)}) collective-permute-start(bf16[48,4096]{1,0:T(8,128)(2,1)S(1)} %pad_maximum_fusion.1), channel_id=1, source_target_pairs={{0,32},{16,48},{32,64},{48,80},{64,96},{80,112},{96,0},{112,16},{1... | collective-permute-start | bytes 1179656 | tf_op jit(solution)/shard_map/ppermute | solution.py:541
  279.6 23.9 %collective-permute-start.9 = (bf16[48,4096]{1,0:T(8,128)(2,1)S(1)}, bf16[48,4096]{1,0:T(8,128)(2,1)S(1)}, u32[]{:S(2)}, u32[]{:S(2)}) collective-permute-start(bf16[48,4096]{1,0:T(8,128)(2,1)S(1)} %pad_maximum_fusion.2), channel_id=1, source_target_pairs={{0,96},{16,112},{32,0},{48,16},{64,32},{80,48},{96,64},{112,80},{1... | collective-permute-start | bytes 1179656 | tf_op jit(solution)/shard_map/ppermute | solution.py:541
  305.9 1.7 copy-start.2
Sparse Core Ops, SparseCore 0:
  269.2 36.6 all-gather.1

commit v4 on v3

--- a/solution.py
+++ b/solution.py
@@ -9,6 +9,8 @@
 HEADS = 4
 MAXLEN = 768
 EPS = 1e-06
+GROUP = 16
+STEPS = 4
 BF = jnp.bfloat16
 F32 = jnp.float32
 NN = (((1,), (0,)), ((), ()))
@@ -28,7 +30,7 @@
     return jnp.where(cond, 1.0, 0.0).astype(BF)
 
 
-def route_kernel(own_ref, loc_ref, slot_ref, req_ref, *, owners, capacity, dummy):
+def route_kernel(own_ref, loc_ref, slot_ref, req_ref, *, owners, capacity, dummy, width):
     lanes = 128
     rows = slot_ref.shape[0]
 
@@ -72,7 +74,7 @@
     high = found[0:owners].astype(jnp.int32)
     low = found[owners : 2 * owners].astype(jnp.int32)
     used = found[2 * owners :] > 0.5
-    req_ref[...] = jnp.where(used, high * 256 + low, dummy)
+    req_ref[...] = jnp.where(used, high * 256 + low, dummy) * (width // 128)
 
 
 def gather_kernel(ids_ref, table_ref, out_ref, wide, picked):
@@ -96,11 +98,12 @@
         wide[rows * parts : rows * parts + 8, :] = jnp.zeros((8, 128), F32)
 
     def copy_rows(k, carry):
+        base = step * count + k * 16
+        taken = k * (16 * parts)
         for u in range(16):
-            s = k * 16 + u
-            row = ids_ref[step * count + s]
-            picked[pl.ds(pl.multiple_of(s * parts, parts), parts), :] = wide[
-                pl.ds(pl.multiple_of(row * parts, parts), parts), :
+            row = ids_ref[base + u]
+            picked[pl.ds(pl.multiple_of(taken + u * parts, parts), parts), :] = wide[
+                pl.ds(pl.multiple_of(row, parts), parts), :
             ]
         return carry
 
@@ -111,10 +114,10 @@
 
 def scatter_kernel(ids_ref, cnt_ref, grad_ref, keep_ref, give_ref, total, rows_in):
     step = pl.program_id(0)
-    count, width = grad_ref.shape
+    sources, count, width = grad_ref.shape
     used = width // 128
     half, rows = keep_ref.shape
-    parts = rows_in.shape[0] // count
+    parts = rows_in.shape[0] // (sources * count)
 
     @pl.when(step == 0)
     def _():
@@ -124,20 +127,37 @@
 
         lax.fori_loop(0, rows * parts // 256, clear, 0)
 
-    for c in range(used):
-        rows_in[pl.ds(c, count, stride=parts), :] = grad_ref[:, c * 128 : (c + 1) * 128].astype(F32)
-
-    def add_rows(k, carry):
-        for u in range(8):
-            s = k * 8 + u
-            row = ids_ref[step * count + s]
-            at = pl.ds(pl.multiple_of(row * parts, parts), parts)
-            total[at, :] = (
-                total[at, :] + rows_in[pl.ds(pl.multiple_of(s * parts, parts), parts), :]
-            )
-        return carry
-
-    lax.fori_loop(0, (cnt_ref[step] + 7) // 8, add_rows, 0)
+    for q in range(sources):
+        for c in range(used):
+            rows_in[pl.ds(q * count * parts + c, count, stride=parts), :] = grad_ref[
+                q, :, c * 128 : (c + 1) * 128
+            ].astype(F32)
+
+    def add_rows(q, k):
+        base = (step * sources + q) * count + k * GROUP
+        taken = (q * count + k * GROUP) * parts
+        for u in range(0, GROUP, 2):
+            one = ids_ref[base + u]
+            two = ids_ref[base + (u + 1)]
+            first = pl.ds(pl.multiple_of(one, parts), parts)
+            second = pl.ds(pl.multiple_of(two, parts), parts)
+            left = rows_in[pl.ds(pl.multiple_of(taken + u * parts, parts), parts), :]
+            right = rows_in[pl.ds(pl.multiple_of(taken + (u + 1) * parts, parts), parts), :]
+            both = jnp.where(one == two, 1.0, 0.0)
+            sum_one = total[first, :] + left
+            sum_two = total[second, :] + (right + left * both)
+            total[first, :] = sum_one
+            total[second, :] = sum_two
+
+    def add_source(q, carry):
+        def group(k, inner):
+            add_rows(q, k)
+            return inner
+
+        lax.fori_loop(0, (cnt_ref[step * sources + q] + (GROUP - 1)) // GROUP, group, 0)
+        return carry
+
+    lax.fori_loop(0, sources, add_source, 0)
 
     @pl.when(step == pl.num_programs(0) - 1)
     def _():
@@ -406,9 +426,9 @@
     return pltpu.CompilerParams(vmem_limit_bytes=mib * 2**20, **more)
 
 
-def route(own, loc, capacity, owners, dummy):
+def route(own, loc, capacity, owners, dummy, width):
     return pl.pallas_call(
-        lambda *refs: route_kernel(*refs, owners=owners, capacity=capacity, dummy=dummy),
+        lambda *refs: route_kernel(*refs, owners=owners, capacity=capacity, dummy=dummy, width=width),
         out_shape=(
             jax.ShapeDtypeStruct((own.size // 128, 128), jnp.int32),
             jax.ShapeDtypeStruct((owners, capacity), jnp.int32),
@@ -439,20 +459,21 @@
 def gather_rows(ids, table, owners, capacity):
     rows, width = table.shape
     parts = width // 128
+    block = owners * capacity // STEPS
     return pl.pallas_call(
         gather_kernel,
         out_shape=jax.ShapeDtypeStruct((owners * capacity, width), BF),
         grid_spec=pltpu.PrefetchScalarGridSpec(
             num_scalar_prefetch=1,
-            grid=(owners,),
+            grid=(STEPS,),
             in_specs=[pl.BlockSpec((rows, width), lambda i, ids: (0, 0))],
-            out_specs=pl.BlockSpec((capacity, width), lambda i, ids: (i, 0)),
+            out_specs=pl.BlockSpec((block, width), lambda i, ids: (i, 0)),
             scratch_shapes=[
                 pltpu.VMEM(((rows + 2) * parts, 128), F32),
-                pltpu.VMEM((capacity * parts, 128), F32),
+                pltpu.VMEM((block * parts, 128), F32),
             ],
         ),
-        compiler_params=params(32),
+        compiler_params=params(56),
         name="gather_rows",
     )(ids, table)
 
@@ -460,17 +481,18 @@
 def scatter_rows(ids, counts, grads, rows, owners, capacity):
     width = grads.shape[2]
     parts = 1 if width == 128 else 4
+    sources = owners // STEPS if parts == 1 else 1
     return pl.pallas_call(
         scatter_kernel,
         out_shape=(jax.ShapeDtypeStruct((width // 2, rows), BF),) * 2,
         grid_spec=pltpu.PrefetchScalarGridSpec(
             num_scalar_prefetch=2,
-            grid=(owners,),
-            in_specs=[pl.BlockSpec((None, capacity, width), lambda i, *_: (i, 0, 0))],
+            grid=(owners // sources,),
+            in_specs=[pl.BlockSpec((sources, capacity, width), lambda i, *_: (i, 0, 0))],
             out_specs=(pl.BlockSpec((width // 2, rows), lambda i, *_: (0, 0)),) * 2,
             scratch_shapes=[
                 pltpu.VMEM(((rows + 8) * parts, 128), F32),
-                pltpu.VMEM((capacity * parts, 128), F32),
+                pltpu.VMEM((sources * capacity * parts, 128), F32),
             ],
         ),
         compiler_params=params(40),
@@ -574,10 +596,10 @@
     lookups = events * lookups_each
     capacity = 2 * lookups // owners
     wide = w_in.shape[1]
-    slots, requests = route(owner.T, local_row.T, capacity, owners, rows_owned)
+    slots, requests = route(owner.T, local_row.T, capacity, owners, rows_owned, width)
     asked = lax.all_to_all(requests, "table", split_axis=0, concat_axis=0, tiled=True)
     ids = asked.reshape(owners * capacity)
-    counts = jnp.sum((asked < rows_owned).astype(jnp.int32), axis=1)
+    counts = jnp.sum((asked < rows_owned * (width // 128)).astype(jnp.int32), axis=1)
     found = gather_rows(ids, table, owners, capacity)
     found = found.reshape(owners, capacity, width)
     arrived = lax.all_to_all(found, "table", split_axis=0, concat_axis=0, tiled=True)
@@ -590,7 +612,8 @@
         return lax.all_to_all(value, "table", split_axis=0, concat_axis=0, tiled=True)
 
     def scatter(value):
-        return scatter_rows(ids, counts, value, rows_owned, owners, capacity)
+        at = ids if value.shape[2] > 128 else ids // (width // 128)
+        return scatter_rows(at, counts, value, rows_owned, owners, capacity)
 
     both = wide + width
     got_a = exchange(send_a.reshape(owners, capacity, -1))

time: 319 us -> 309 us (0.969)
  local copies, waits for them, and re-layouts: 10.3 us -> 6.07 us
  Pallas kernels: 95.1 us -> 91 us
    pallas_call x2, Pallas kernels: 24.8 us -> 19.1 us  [scatter_rows(): pl.pallas_call(scatter_kernel, out_shape=(jax.ShapeDtypeStruct((width //...]
    unnamed x10 -> x8, local copies, waits for them, and re-layouts: 7.1 us -> 2.92 us
  transfers between devices with their start and end apart: 18 -> 18, of which waited for: 11 -> 11; matrix products, arithmetic and copies ran while one was open for 4% -> 4% of each run, Pallas kernels for 8% -> 6%
where the time goes in v4:
time: 309 us; the launch traced here: 308 us
  waiting for transfers between devices  109 us (35%)
  Pallas kernels  91 us (29%)
  starting transfers between devices  46.8 us (15%)
  blocking collectives  30.5 us (10%)
  between operations  14.2 us (5%)
  other arithmetic  9.69 us (3%)
  local copies, waits for them, and re-layouts  6.07 us (2%)
    all_to_all x1, waiting for transfers between devices, whole(): lax.all_to_all(found, 'table', split_axis=0, concat_axis=0, tiled=True)  51.5 us
    pallas_call x1, Pallas kernels, layer(): pl.pallas_call(layer_kernel, in_specs=[pl.BlockSpec(memory_space=pltpu.SM...  46.6 us
    ppermute x11, waiting for transfers between devices, along_z(): lax.ppermute(value, 'dp', [(d, (d // 2 + hop) % 4 * 2 + d % 2) for d in r...  33 us
    all_to_all x2, waiting for transfers between devices, exchange(): lax.all_to_all(value, 'table', split_axis=0, concat_axis=0, tiled=True)  23.8 us
    pallas_call x2, Pallas kernels, scatter_rows(): pl.pallas_call(scatter_kernel, out_shape=(jax.ShapeDtypeStruct((width //...  19.1 us
    ppermute x11, starting transfers between devices, along_z(): lax.ppermute(value, 'dp', [(d, (d // 2 + hop) % 4 * 2 + d % 2) for d in r...  16.8 us
    all_to_all x1, blocking collectives, exchange(): lax.all_to_all(value, 'table', split_axis=0, concat_axis=0, tiled=True)  16.7 us
    all_to_all x2, starting transfers between devices, exchange(): lax.all_to_all(value, 'table', split_axis=0, concat_axis=0, tiled=True)  15.7 us
  transfers between devices with their start and end apart: 18, of which 11 were waited for; matrix products, arithmetic and copies ran while one was open for 4% of the time, Pallas kernels for 6%

profile of v4, /device:TPU:1, one launch (start us, length us, event | category | flops | bytes accessed | tf_op | source)
XLA Modules:
  0.0 307.8 jit_solution(1860213890401380998)
XLA Ops:
  7.2 2.1 route.1
  10.0 13.8 %all_to_all.29 = s32[16,1,256]{2,1,0:T(1,128)} all-to-all(s32[16,1,256]{2,1,0:T(1,128)S(1)} %copy.11), channel_id=1, replica_groups=mesh['dp'=8,'table'=16] {'table'}, dimensions={0} | all-to-all | bytes 32768 | tf_op jit(solution)/shard_map/all_to_all | solution.py:600
  23.8 10.6 %gather_rows.1 = bf16[4096,512]{1,0:T(8,128)(2,1)} custom-call(s32[4096]{0:T(1024)} %bitcast.11, bf16[4096,512]{1,0:T(8,128)(2,1)} %table_ref.1), custom_call_target="tpu_custom_call" | custom-call | tf_op jit(solution)/shard_map/gather_rows/pallas_call | solution.py:463
  34.4 4.5 %all-to-all-start.1 = ((bf16[16,256,512]{2,1,0:T(8,128)(2,1)}), bf16[16,256,512]{2,1,0:T(8,128)(2,1)}, u32[]{:S(2)}, u32[]{:S(2)}) async-start(bf16[16,256,512]{2,1,0:T(8,128)(2,1)} %bitcast.14), calls=%async_computation.1 | async-start | bytes 8388608 | tf_op jit(solution)/shard_map/all_to_all | solution.py:605
  39.0 51.5 %all-to-all-done.1 = bf16[16,256,512]{2,1,0:T(8,128)(2,1)} async-done(((bf16[16,256,512]{2,1,0:T(8,128)(2,1)}), bf16[16,256,512]{2,1,0:T(8,128)(2,1)}, u32[]{:S(2)}, u32[]{:S(2)}) %all-to-all-start.1) | async-done | bytes 4194336 | tf_op jit(solution)/shard_map/all_to_all | solution.py:605
  90.5 46.6 %layer.1 = (bf16[1024,512]{1,0:T(8,128)(2,1)}, bf16[4096,384]{1,0:T(8,128)(2,1)}, bf16[4096,128]{1,0:T(8,128)(2,1)}, bf16[1024,512]{1,0:T(8,128)(2,1)}, bf16[102...) custom-call(s32[1]{0:T(128)} %bitcast.place_ref, bf16[4096,512]{1,0:T(8,128)(2,1)} %bitcast.6.arrived_ref, ...), custom_call_target="tpu_custom_call" | custom-call | tf_op jit(solution)/shard_map/layer/pallas_call | solution.py:509
  137.1 8.9 %weight_grads.1 = (bf16[256,2560]{1,0:T(8,128)(2,1)}, bf16[256,2560]{1,0:T(8,128)(2,1)}) custom-call(s32[1]{0:T(128)} %bitcast.place_ref, bf16[1024,512]{1,0:T(8,128)(2,1)} %get-tuple-element.24.normed_ref, bf16[1024,2048]{1,0:T(8,128)(2,1)} %get-tuple-element.25.du_ref, bf16[1024,512]{1,0:T(8,128)(2,1)} %get-tuple-element.26.gated_ref, bf16[1024,512]{1,0:T(8,128)(2,1)} %og_ref.3), custom_call_target="tpu_custom_call" | custom-call | tf_op jit(solution)/shard_map/weight_grads/pallas_call | solution.py:540
  146.0 5.2 %collective-permute-start = (bf16[256,2560]{1,0:T(8,128)(2,1)}, bf16[256,2560]{1,0:T(8,128)(2,1)}, u32[]{:S(2)}, u32[]{:S(2)}) collective-permute-start(bf16[256,2560]{1,0:T(8,128)(2,1)} %get-tuple-element.28), channel_id=1, source_target_pairs={{0,16},{16,0},{32,48},{48,32},{64,80},{80,64},{96,112},{112,96},{1... | collective-permute-start | bytes 3932168 | tf_op jit(solution)/shard_map/ppermute | solution.py:559
  151.1 4.0 %all-to-all-start.4 = ((bf16[16,256,384]{2,1,0:T(8,128)(2,1)}), bf16[16,256,384]{2,1,0:T(8,128)(2,1)S(1)}, u32[]{:S(2)}, u32[]{:S(2)}) async-start(bf16[16,256,384]{2,1,0:T(8,128)(2,1)} %bitcast.15), calls=%async_computation.4 | async-start | bytes 6291456 | tf_op jit(solution)/shard_map/all_to_all | solution.py:612
  155.2 2.0 add_convert_fusion.1
  157.3 1.7 collective-permute-start.1
  159.0 2.2 collective-permute-start.3
  161.2 4.2 %collective-permute-done.1 = bf16[32,2560]{1,0:T(8,128)(2,1)S(1)} collective-permute-done((bf16[32,2560]{1,0:T(8,128)(2,1)S(1)}, bf16[32,2560]{1,0:T(8,128)(2,1)S(1)}, u32[]{:S(2)}, u32[]{:S(2)}) %collective-permute-start.1) | collective-permute-done | bytes 163872 | tf_op jit(solution)/shard_map/ppermute | solution.py:563
  166.0 2.3 collective-permute-start.4
  168.3 6.8 %collective-permute-done.2 = bf16[64,2560]{1,0:T(8,128)(2,1)S(1)} collective-permute-done((bf16[64,2560]{1,0:T(8,128)(2,1)S(1)}, bf16[64,2560]{1,0:T(8,128)(2,1)S(1)}, u32[]{:S(2)}, u32[]{:S(2)}) %collective-permute-start.2) | collective-permute-done | bytes 327712 | tf_op jit(solution)/shard_map/ppermute | solution.py:563
  176.5 2.5 pad_maximum_fusion
  179.0 17.6 %all-to-all-done.4.grad_ref = bf16[16,256,384]{2,1,0:T(8,128)(2,1)S(1)} async-done(((bf16[16,256,384]{2,1,0:T(8,128)(2,1)}), bf16[16,256,384]{2,1,0:T(8,128)(2,1)S(1)}, u32[]{:S(2)}, u32[]{:S(2)}) %all-to-all-start.4) | async-done | bytes 3145760 | tf_op jit(solution)/shard_map/all_to_all | solution.py:612
  196.6 11.7 %all-to-all-start.2 = ((bf16[16,336,128]{2,1,0:T(8,128)(2,1)}), bf16[16,336,128]{2,1,0:T(8,128)(2,1)}, u32[]{:S(2)}, u32[]{:S(2)}) async-start(bf16[16,336,128]{2,1,0:T(8,128)(2,1)} %pad_maximum_fusion), calls=%async_computation.2 | async-start | bytes 2752512 | tf_op jit(solution)/shard_map/all_to_all | solution.py:612
  208.7 10.0 %scatter_rows.2 = (bf16[192,4096]{1,0:T(8,128)(2,1)S(1)}, bf16[192,4096]{1,0:T(8,128)(2,1)}) custom-call(s32[4096]{0:T(1024)S(1)} %bitcast.12, s32[16]{0:T(128)S(1)} %fusion.1.cnt_ref, bf16[16,256,384]{2,1,0:T(8,128)(2,1)S(1)} %all-to-all-done.4.grad_ref), custom_call_target="tpu_custom_call" | custom-call | tf_op jit(solution)/shard_map/scatter_rows/pallas_call | solution.py:485
  221.0 6.2 %all-to-all-done.2.grad_ref = bf16[16,336,128]{2,1,0:T(8,128)(2,1)} async-done(((bf16[16,336,128]{2,1,0:T(8,128)(2,1)}), bf16[16,336,128]{2,1,0:T(8,128)(2,1)}, u32[]{:S(2)}, u32[]{:S(2)}) %all-to-all-start.2) | async-done | bytes 1376288 | tf_op jit(solution)/shard_map/all_to_all | solution.py:612
  227.2 9.1 %scatter_rows.3 = (bf16[64,4096]{1,0:T(8,128)(2,1)S(1)}, bf16[64,4096]{1,0:T(8,128)(2,1)S(1)}) custom-call(s32[4096]{0:T(1024)S(1)} %add_select_fusion.ids_ref, s32[16]{0:T(128)S(1)} %fusion.1.cnt_ref, bf16[16,336,128]{2,1,0:T(8,128)(2,1)} %all-to-all-done.2.grad_ref), custom_call_target="tpu_custom_call" | custom-call | tf_op jit(solution)/shard_map/scatter_rows/pallas_call | solution.py:485
  236.3 3.5 %collective-permute-start.10 = (bf16[64,4096]{1,0:T(8,128)(2,1)S(1)}, bf16[64,4096]{1,0:T(8,128)(2,1)S(1)}, u32[]{:S(2)}, u32[]{:S(2)}) collective-permute-start(bf16[64,4096]{1,0:T(8,128)(2,1)S(1)} %get-tuple-element.35), channel_id=1, source_target_pairs={{0,16},{16,0},{32,48},{48,32},{64,80},{80,64},{96,112},{112,96},{1... | collective-permute-start | bytes 1572872 | tf_op jit(solution)/shard_map/ppermute | solution.py:559
  240.8 16.7 %all_to_all.30 = bf16[16,80,128]{2,1,0:T(8,128)(2,1)S(1)} all-to-all(bf16[16,80,128]{2,1,0:T(8,128)(2,1)S(1)} %broadcast_in_dim.2), channel_id=1, replica_groups=mesh['dp'=8,'table'=16] {'table'}, dimensions={0} | all-to-all | bytes 655360 | tf_op jit(solution)/shard_map/all_to_all | solution.py:612
  258.9 1.9 add_convert_fusion
  262.6 2.2 collective-permute-start.8
  264.9 2.6 collective-permute-start.12
  269.3 1.9 collective-permute-start.9
  271.8 2.7 collective-permute-done.12
  276.3 13.7 %collective-permute-done.7 = bf16[48,4096]{1,0:T(8,128)(2,1)S(1)} collective-permute-done((bf16[48,4096]{1,0:T(8,128)(2,1)S(1)}, bf16[48,4096]{1,0:T(8,128)(2,1)S(1)}, u32[]{:S(2)}, u32[]{:S(2)}) %collective-permute-start.7) | collective-permute-done | bytes 393248 | tf_op jit(solution)/shard_map/ppermute | solution.py:563
  290.0 3.2 %collective-permute-done.9 = bf16[48,4096]{1,0:T(8,128)(2,1)S(1)} collective-permute-done((bf16[48,4096]{1,0:T(8,128)(2,1)S(1)}, bf16[48,4096]{1,0:T(8,128)(2,1)S(1)}, u32[]{:S(2)}, u32[]{:S(2)}) %collective-permute-start.9) | collective-permute-done | bytes 393248 | tf_op jit(solution)/shard_map/ppermute | solution.py:563
  295.5 1.7 copy-done
  297.3 3.7 %finish.1 = (f32[512,2048]{1,0:T(8,128)}, f32[512,512]{1,0:T(8,128)}) custom-call(bf16[512,2560]{1,0:T(8,128)(2,1)S(1)} %copy-done), custom_call_target="tpu_custom_call" | custom-call | tf_op jit(solution)/shard_map/finish/pallas_call | solution.py:442
  (46 shorter events, 16.1 us)
Async XLA Ops:
  34.4 56.1 %all-to-all-start.1 = ((bf16[16,256,512]{2,1,0:T(8,128)(2,1)}), bf16[16,256,512]{2,1,0:T(8,128)(2,1)}, u32[]{:S(2)}, u32[]{:S(2)}) async-start(bf16[16,256,512]{2,1,0:T(8,128)(2,1)} %bitcast.14), calls=%async_computation.1 | async-start | bytes 8388608 | tf_op jit(solution)/shard_map/all_to_all | solution.py:605
  146.0 9.2 %collective-permute-start = (bf16[256,2560]{1,0:T(8,128)(2,1)}, bf16[256,2560]{1,0:T(8,128)(2,1)}, u32[]{:S(2)}, u32[]{:S(2)}) collective-permute-start(bf16[256,2560]{1,0:T(8,128)(2,1)} %get-tuple-element.28), channel_id=1, source_target_pairs={{0,16},{16,0},{32,48},{48,32},{64,80},{80,64},{96,112},{112,96},{1... | collective-permute-start | bytes 3932168 | tf_op jit(solution)/shard_map/ppermute | solution.py:559
  151.1 45.5 %all-to-all-start.4 = ((bf16[16,256,384]{2,1,0:T(8,128)(2,1)}), bf16[16,256,384]{2,1,0:T(8,128)(2,1)S(1)}, u32[]{:S(2)}, u32[]{:S(2)}) async-start(bf16[16,256,384]{2,1,0:T(8,128)(2,1)} %bitcast.15), calls=%async_computation.4 | async-start | bytes 6291456 | tf_op jit(solution)/shard_map/all_to_all | solution.py:612
  157.3 8.1 %collective-permute-start.1 = (bf16[32,2560]{1,0:T(8,128)(2,1)S(1)}, bf16[32,2560]{1,0:T(8,128)(2,1)S(1)}, u32[]{:S(2)}, u32[]{:S(2)}) collective-permute-start(bf16[32,2560]{1,0:T(8,128)(2,1)S(1)} %get-tuple-element.44), channel_id=1, source_target_pairs={{0,32},{16,48},{32,64},{48,80},{64,96},{80,112},{96,0},{112,16},{1... | collective-permute-start | bytes 491528 | tf_op jit(solution)/shard_map/ppermute | solution.py:563
  159.0 6.4 %collective-permute-start.3 = (bf16[32,2560]{1,0:T(8,128)(2,1)S(1)}, bf16[32,2560]{1,0:T(8,128)(2,1)S(1)}, u32[]{:S(2)}, u32[]{:S(2)}) collective-permute-start(bf16[32,2560]{1,0:T(8,128)(2,1)S(1)} %get-tuple-element.45), channel_id=1, source_target_pairs={{0,96},{16,112},{32,0},{48,16},{64,32},{80,48},{96,64},{112,80},{1... | collective-permute-start | bytes 491528 | tf_op jit(solution)/shard_map/ppermute | solution.py:563
  165.5 9.7 %collective-permute-start.2 = (bf16[64,2560]{1,0:T(8,128)(2,1)S(1)}, bf16[64,2560]{1,0:T(8,128)(2,1)S(1)}, u32[]{:S(2)}, u32[]{:S(2)}) collective-permute-start(bf16[64,2560]{1,0:T(8,128)(2,1)S(1)} %pad_maximum_fusion.3), channel_id=1, source_target_pairs={{0,32},{16,48},{32,64},{48,80},{64,96},{80,112},{96,0},{112,16},{1... | collective-permute-start | bytes 983048 | tf_op jit(solution)/shard_map/ppermute | solution.py:563
  166.0 9.2 %collective-permute-start.4 = (bf16[64,2560]{1,0:T(8,128)(2,1)S(1)}, bf16[64,2560]{1,0:T(8,128)(2,1)S(1)}, u32[]{:S(2)}, u32[]{:S(2)}) collective-permute-start(bf16[64,2560]{1,0:T(8,128)(2,1)S(1)} %pad_maximum_fusion.4), channel_id=1, source_target_pairs={{0,96},{16,112},{32,0},{48,16},{64,32},{80,48},{96,64},{112,80},{1... | collective-permute-start | bytes 983048 | tf_op jit(solution)/shard_map/ppermute | solution.py:563
  179.0 29.3 %copy-start.3 = (s32[16,1,256]{2,1,0:T(1,128)S(1)}, s32[16,1,256]{2,1,0:T(1,128)}, u32[]{:S(2)}) copy-start(s32[16,1,256]{2,1,0:T(1,128)} %all_to_all.29) | copy-start | bytes 49156
  196.6 30.6 %all-to-all-start.2 = ((bf16[16,336,128]{2,1,0:T(8,128)(2,1)}), bf16[16,336,128]{2,1,0:T(8,128)(2,1)}, u32[]{:S(2)}, u32[]{:S(2)}) async-start(bf16[16,336,128]{2,1,0:T(8,128)(2,1)} %pad_maximum_fusion), calls=%async_computation.2 | async-start | bytes 2752512 | tf_op jit(solution)/shard_map/all_to_all | solution.py:612
  208.3 87.2 %all-gather.2.cloned.1.call-start = ((), (), s32[]{:S(2)}) async-start(), calls=%async_computation.5 | async-start | bytes 2949120 | tf_op jit(solution)/shard_map/all_gather | solution.py:632
  218.8 1.2 copy-start.1
  219.9 38.9 %collective-permute-start.5 = (bf16[192,4096]{1,0:T(8,128)(2,1)}, bf16[192,4096]{1,0:T(8,128)(2,1)}, u32[]{:S(2)}, u32[]{:S(2)}) collective-permute-start(bf16[192,4096]{1,0:T(8,128)(2,1)} %get-tuple-element.33), channel_id=1, source_target_pairs={{0,16},{16,0},{32,48},{48,32},{64,80},{80,64},{96,112},{112,96},{1... | collective-permute-start | bytes 4718600 | tf_op jit(solution)/shard_map/ppermute | solution.py:559
  236.3 22.5 %collective-permute-start.10 = (bf16[64,4096]{1,0:T(8,128)(2,1)S(1)}, bf16[64,4096]{1,0:T(8,128)(2,1)S(1)}, u32[]{:S(2)}, u32[]{:S(2)}) collective-permute-start(bf16[64,4096]{1,0:T(8,128)(2,1)S(1)} %get-tuple-element.35), channel_id=1, source_target_pairs={{0,16},{16,0},{32,48},{48,32},{64,80},{80,64},{96,112},{112,96},{1... | collective-permute-start | bytes 1572872 | tf_op jit(solution)/shard_map/ppermute | solution.py:559
  240.8 18.0 %copy-start.2 = (bf16[192,4096]{1,0:T(8,128)(2,1)S(1)}, bf16[192,4096]{1,0:T(8,128)(2,1)}, u32[]{:S(2)}) copy-start(bf16[192,4096]{1,0:T(8,128)(2,1)} %copy-done.1) | copy-start | bytes 4718596
  260.9 7.3 %collective-permute-start.6 = (bf16[24,4096]{1,0:T(8,128)(2,1)S(1)}, bf16[24,4096]{1,0:T(8,128)(2,1)S(1)}, u32[]{:S(2)}, u32[]{:S(2)}) collective-permute-start(bf16[24,4096]{1,0:T(8,128)(2,1)S(1)} %get-tuple-element.38), channel_id=1, source_target_pairs={{0,32},{16,48},{32,64},{48,80},{64,96},{80,112},{96,0},{112,16},{1... | collective-permute-start | bytes 589832 | tf_op jit(solution)/shard_map/ppermute | solution.py:563
  262.6 5.6 %collective-permute-start.8 = (bf16[24,4096]{1,0:T(8,128)(2,1)S(1)}, bf16[24,4096]{1,0:T(8,128)(2,1)S(1)}, u32[]{:S(2)}, u32[]{:S(2)}) collective-permute-start(bf16[24,4096]{1,0:T(8,128)(2,1)S(1)} %get-tuple-element.39), channel_id=1, source_target_pairs={{0,96},{16,112},{32,0},{48,16},{64,32},{80,48},{96,64},{112,80},{1... | collective-permute-start | bytes 589832 | tf_op jit(solution)/shard_map/ppermute | solution.py:563
  264.8 7.0 %collective-permute-start.11 = (bf16[16,4096]{1,0:T(8,128)(2,1)S(1)}, bf16[16,4096]{1,0:T(8,128)(2,1)S(1)}, u32[]{:S(2)}, u32[]{:S(2)}) collective-permute-start(bf16[16,4096]{1,0:T(8,128)(2,1)S(1)} %get-tuple-element.48), channel_id=1, source_target_pairs={{0,32},{16,48},{32,64},{48,80},{64,96},{80,112},{96,0},{112,16},{1... | collective-permute-start | bytes 393224 | tf_op jit(solution)/shard_map/ppermute | solution.py:563
  264.9 9.6 %collective-permute-start.12 = (bf16[16,4096]{1,0:T(8,128)(2,1)S(1)}, bf16[16,4096]{1,0:T(8,128)(2,1)S(1)}, u32[]{:S(2)}, u32[]{:S(2)}) collective-permute-start(bf16[16,4096]{1,0:T(8,128)(2,1)S(1)} %get-tuple-element.50), channel_id=1, source_target_pairs={{0,64},{16,80},{32,96},{48,112},{64,0},{80,16},{96,32},{112,48},{1... | collective-permute-start | bytes 393224 | tf_op jit(solution)/shard_map/ppermute | solution.py:563
  267.5 8.7 %collective-permute-start.13 = (bf16[16,4096]{1,0:T(8,128)(2,1)S(1)}, bf16[16,4096]{1,0:T(8,128)(2,1)S(1)}, u32[]{:S(2)}, u32[]{:S(2)}) collective-permute-start(bf16[16,4096]{1,0:T(8,128)(2,1)S(1)} %get-tuple-element.49), channel_id=1, source_target_pairs={{0,96},{16,112},{32,0},{48,16},{64,32},{80,48},{96,64},{112,80},{1... | collective-permute-start | bytes 393224 | tf_op jit(solution)/shard_map/ppermute | solution.py:563
  268.3 21.6 %collective-permute-start.7 = (bf16[48,4096]{1,0:T(8,128)(2,1)S(1)}, bf16[48,4096]{1,0:T(8,128)(2,1)S(1)}, u32[]{:S(2)}, u32[]{:S(2)}) collective-permute-start(bf16[48,4096]{1,0:T(8,128)(2,1)S(1)} %pad_maximum_fusion.1), channel_id=1, source_target_pairs={{0,32},{16,48},{32,64},{48,80},{64,96},{80,112},{96,0},{112,16},{1... | collective-permute-start | bytes 1179656 | tf_op jit(solution)/shard_map/ppermute | solution.py:563
  269.3 23.9 %collective-permute-start.9 = (bf16[48,4096]{1,0:T(8,128)(2,1)S(1)}, bf16[48,4096]{1,0:T(8,128)(2,1)S(1)}, u32[]{:S(2)}, u32[]{:S(2)}) collective-permute-start(bf16[48,4096]{1,0:T(8,128)(2,1)S(1)} %pad_maximum_fusion.2), channel_id=1, source_target_pairs={{0,96},{16,112},{32,0},{48,16},{64,32},{80,48},{96,64},{112,80},{1... | collective-permute-start | bytes 1179656 | tf_op jit(solution)/shard_map/ppermute | solution.py:563
  295.5 1.7 copy-start
Sparse Core Ops, SparseCore 0:
  258.8 36.6 all-gather.1

commit v5 on v4

--- a/solution.py
+++ b/solution.py
@@ -9,7 +9,7 @@
 HEADS = 4
 MAXLEN = 768
 EPS = 1e-06
-GROUP = 16
+GROUP = 32
 STEPS = 4
 BF = jnp.bfloat16
 F32 = jnp.float32
@@ -371,7 +371,7 @@
         eg_ref[rows, :] = dot(grad.astype(BF), spread).astype(BF)
         return carry
 
-    steps(last, nblk, 1)
+    steps(last, nblk, 2)
 
     def pack(o, carry):
         where = iota((cap_step, 128), 0) + o * cap_step
@@ -572,7 +572,9 @@
     up = jnp.concatenate([up[:half] + ahead.astype(F32), up[half:]], axis=0).astype(BF)
     down = pieces[3].astype(F32)
     down = jnp.concatenate([down[:half], down[half:] + behind.astype(F32)], axis=0).astype(BF)
-    return pieces[0].astype(F32) + move(up, 1).astype(F32) + move(down, -1).astype(F32)
+    from_up = move(up, 1)
+    from_down = move(down, -1)
+    return pieces[0].astype(F32) + from_up.astype(F32) + from_down.astype(F32)
 
 
 def direct_sum(pieces, move):

time: 309 us -> 308 us (level)
  transfers between devices with their start and end apart: 18 -> 18, of which waited for: 11 -> 11; matrix products, arithmetic and copies ran while one was open for 4% -> 4% of each run, Pallas kernels for 6% -> 7%
where the time goes in v5:
time: 308 us; the launch traced here: 307 us
  waiting for transfers between devices  109 us (35%)
  Pallas kernels  91.8 us (30%)
  starting transfers between devices  45.9 us (15%)
  blocking collectives  29.7 us (10%)
  between operations  14.2 us (5%)
  other arithmetic  9.69 us (3%)
  local copies, waits for them, and re-layouts  6.07 us (2%)
    all_to_all x1, waiting for transfers between devices, whole(): lax.all_to_all(found, 'table', split_axis=0, concat_axis=0, tiled=True)  51.5 us
    pallas_call x1, Pallas kernels, layer(): pl.pallas_call(layer_kernel, in_specs=[pl.BlockSpec(memory_space=pltpu.SM...  46.3 us
    ppermute x11, waiting for transfers between devices, along_z(): lax.ppermute(value, 'dp', [(d, (d // 2 + hop) % 4 * 2 + d % 2) for d in r...  33 us
    all_to_all x2, waiting for transfers between devices, exchange(): lax.all_to_all(value, 'table', split_axis=0, concat_axis=0, tiled=True)  23.6 us
    pallas_call x2, Pallas kernels, scatter_rows(): pl.pallas_call(scatter_kernel, out_shape=(jax.ShapeDtypeStruct((width //...  20.2 us
    ppermute x11, starting transfers between devices, along_z(): lax.ppermute(value, 'dp', [(d, (d // 2 + hop) % 4 * 2 + d % 2) for d in r...  16.8 us
    all_to_all x1, blocking collectives, exchange(): lax.all_to_all(value, 'table', split_axis=0, concat_axis=0, tiled=True)  15.9 us
    all_to_all x2, starting transfers between devices, exchange(): lax.all_to_all(value, 'table', split_axis=0, concat_axis=0, tiled=True)  15.7 us
  transfers between devices with their start and end apart: 18, of which 11 were waited for; matrix products, arithmetic and copies ran while one was open for 4% of the time, Pallas kernels for 7%

profile of v5, /device:TPU:1, one launch (start us, length us, event | category | flops | bytes accessed | tf_op | source)
XLA Modules:
  0.0 306.6 jit_solution(2044433273118496577)
XLA Ops:
  7.2 2.1 route.1
  10.0 13.8 %all_to_all.29 = s32[16,1,256]{2,1,0:T(1,128)} all-to-all(s32[16,1,256]{2,1,0:T(1,128)S(1)} %copy.11), channel_id=1, replica_groups=mesh['dp'=8,'table'=16] {'table'}, dimensions={0} | all-to-all | bytes 32768 | tf_op jit(solution)/shard_map/all_to_all | solution.py:602
  23.8 10.6 %gather_rows.1 = bf16[4096,512]{1,0:T(8,128)(2,1)} custom-call(s32[4096]{0:T(1024)} %bitcast.11, bf16[4096,512]{1,0:T(8,128)(2,1)} %table_ref.1), custom_call_target="tpu_custom_call" | custom-call | tf_op jit(solution)/shard_map/gather_rows/pallas_call | solution.py:463
  34.4 4.5 %all-to-all-start.1 = ((bf16[16,256,512]{2,1,0:T(8,128)(2,1)}), bf16[16,256,512]{2,1,0:T(8,128)(2,1)}, u32[]{:S(2)}, u32[]{:S(2)}) async-start(bf16[16,256,512]{2,1,0:T(8,128)(2,1)} %bitcast.14), calls=%async_computation.1 | async-start | bytes 8388608 | tf_op jit(solution)/shard_map/all_to_all | solution.py:607
  39.0 51.5 %all-to-all-done.1 = bf16[16,256,512]{2,1,0:T(8,128)(2,1)} async-done(((bf16[16,256,512]{2,1,0:T(8,128)(2,1)}), bf16[16,256,512]{2,1,0:T(8,128)(2,1)}, u32[]{:S(2)}, u32[]{:S(2)}) %all-to-all-start.1) | async-done | bytes 4194336 | tf_op jit(solution)/shard_map/all_to_all | solution.py:607
  90.5 46.3 %layer.1 = (bf16[1024,512]{1,0:T(8,128)(2,1)}, bf16[4096,384]{1,0:T(8,128)(2,1)}, bf16[4096,128]{1,0:T(8,128)(2,1)}, bf16[1024,512]{1,0:T(8,128)(2,1)}, bf16[102...) custom-call(s32[1]{0:T(128)} %bitcast.place_ref, bf16[4096,512]{1,0:T(8,128)(2,1)} %bitcast.6.arrived_ref, ...), custom_call_target="tpu_custom_call" | custom-call | tf_op jit(solution)/shard_map/layer/pallas_call | solution.py:509
  136.7 8.9 %weight_grads.1 = (bf16[256,2560]{1,0:T(8,128)(2,1)}, bf16[256,2560]{1,0:T(8,128)(2,1)}) custom-call(s32[1]{0:T(128)} %bitcast.place_ref, bf16[1024,512]{1,0:T(8,128)(2,1)} %get-tuple-element.24.normed_ref, bf16[1024,2048]{1,0:T(8,128)(2,1)} %get-tuple-element.25.du_ref, bf16[1024,512]{1,0:T(8,128)(2,1)} %get-tuple-element.26.gated_ref, bf16[1024,512]{1,0:T(8,128)(2,1)} %og_ref.3), custom_call_target="tpu_custom_call" | custom-call | tf_op jit(solution)/shard_map/weight_grads/pallas_call | solution.py:540
  145.6 5.2 %collective-permute-start = (bf16[256,2560]{1,0:T(8,128)(2,1)}, bf16[256,2560]{1,0:T(8,128)(2,1)}, u32[]{:S(2)}, u32[]{:S(2)}) collective-permute-start(bf16[256,2560]{1,0:T(8,128)(2,1)} %get-tuple-element.28), channel_id=1, source_target_pairs={{0,16},{16,0},{32,48},{48,32},{64,80},{80,64},{96,112},{112,96},{1... | collective-permute-start | bytes 3932168 | tf_op jit(solution)/shard_map/ppermute | solution.py:559
  150.8 4.0 %all-to-all-start.4 = ((bf16[16,256,384]{2,1,0:T(8,128)(2,1)}), bf16[16,256,384]{2,1,0:T(8,128)(2,1)S(1)}, u32[]{:S(2)}, u32[]{:S(2)}) async-start(bf16[16,256,384]{2,1,0:T(8,128)(2,1)} %bitcast.15), calls=%async_computation.4 | async-start | bytes 6291456 | tf_op jit(solution)/shard_map/all_to_all | solution.py:614
  154.8 2.0 add_convert_fusion.1
  156.9 1.7 collective-permute-start.1
  158.6 2.2 collective-permute-start.3
  160.8 4.2 %collective-permute-done.1 = bf16[32,2560]{1,0:T(8,128)(2,1)S(1)} collective-permute-done((bf16[32,2560]{1,0:T(8,128)(2,1)S(1)}, bf16[32,2560]{1,0:T(8,128)(2,1)S(1)}, u32[]{:S(2)}, u32[]{:S(2)}) %collective-permute-start.1) | collective-permute-done | bytes 163872 | tf_op jit(solution)/shard_map/ppermute | solution.py:563
  165.7 2.3 collective-permute-start.4
  168.0 6.8 %collective-permute-done.2 = bf16[64,2560]{1,0:T(8,128)(2,1)S(1)} collective-permute-done((bf16[64,2560]{1,0:T(8,128)(2,1)S(1)}, bf16[64,2560]{1,0:T(8,128)(2,1)S(1)}, u32[]{:S(2)}, u32[]{:S(2)}) %collective-permute-start.2) | collective-permute-done | bytes 327712 | tf_op jit(solution)/shard_map/ppermute | solution.py:563
  176.1 2.5 pad_maximum_fusion
  178.6 17.6 %all-to-all-done.4.grad_ref = bf16[16,256,384]{2,1,0:T(8,128)(2,1)S(1)} async-done(((bf16[16,256,384]{2,1,0:T(8,128)(2,1)}), bf16[16,256,384]{2,1,0:T(8,128)(2,1)S(1)}, u32[]{:S(2)}, u32[]{:S(2)}) %all-to-all-start.4) | async-done | bytes 3145760 | tf_op jit(solution)/shard_map/all_to_all | solution.py:614
  196.3 11.7 %all-to-all-start.2 = ((bf16[16,336,128]{2,1,0:T(8,128)(2,1)}), bf16[16,336,128]{2,1,0:T(8,128)(2,1)}, u32[]{:S(2)}, u32[]{:S(2)}) async-start(bf16[16,336,128]{2,1,0:T(8,128)(2,1)} %pad_maximum_fusion), calls=%async_computation.2 | async-start | bytes 2752512 | tf_op jit(solution)/shard_map/all_to_all | solution.py:614
  208.4 10.7 %scatter_rows.2 = (bf16[192,4096]{1,0:T(8,128)(2,1)S(1)}, bf16[192,4096]{1,0:T(8,128)(2,1)}) custom-call(s32[4096]{0:T(1024)S(1)} %bitcast.12, s32[16]{0:T(128)S(1)} %fusion.1.cnt_ref, bf16[16,256,384]{2,1,0:T(8,128)(2,1)S(1)} %all-to-all-done.4.grad_ref), custom_call_target="tpu_custom_call" | custom-call | tf_op jit(solution)/shard_map/scatter_rows/pallas_call | solution.py:485
  220.8 6.0 %all-to-all-done.2.grad_ref = bf16[16,336,128]{2,1,0:T(8,128)(2,1)} async-done(((bf16[16,336,128]{2,1,0:T(8,128)(2,1)}), bf16[16,336,128]{2,1,0:T(8,128)(2,1)}, u32[]{:S(2)}, u32[]{:S(2)}) %all-to-all-start.2) | async-done | bytes 1376288 | tf_op jit(solution)/shard_map/all_to_all | solution.py:614
  226.8 9.6 %scatter_rows.3 = (bf16[64,4096]{1,0:T(8,128)(2,1)S(1)}, bf16[64,4096]{1,0:T(8,128)(2,1)S(1)}) custom-call(s32[4096]{0:T(1024)S(1)} %add_select_fusion.ids_ref, s32[16]{0:T(128)S(1)} %fusion.1.cnt_ref, bf16[16,336,128]{2,1,0:T(8,128)(2,1)} %all-to-all-done.2.grad_ref), custom_call_target="tpu_custom_call" | custom-call | tf_op jit(solution)/shard_map/scatter_rows/pallas_call | solution.py:485
  236.4 3.1 %collective-permute-start.10 = (bf16[64,4096]{1,0:T(8,128)(2,1)S(1)}, bf16[64,4096]{1,0:T(8,128)(2,1)S(1)}, u32[]{:S(2)}, u32[]{:S(2)}) collective-permute-start(bf16[64,4096]{1,0:T(8,128)(2,1)S(1)} %get-tuple-element.35), channel_id=1, source_target_pairs={{0,16},{16,0},{32,48},{48,32},{64,80},{80,64},{96,112},{112,96},{1... | collective-permute-start | bytes 1572872 | tf_op jit(solution)/shard_map/ppermute | solution.py:559
  240.6 15.9 %all_to_all.30 = bf16[16,80,128]{2,1,0:T(8,128)(2,1)S(1)} all-to-all(bf16[16,80,128]{2,1,0:T(8,128)(2,1)S(1)} %broadcast_in_dim.2), channel_id=1, replica_groups=mesh['dp'=8,'table'=16] {'table'}, dimensions={0} | all-to-all | bytes 655360 | tf_op jit(solution)/shard_map/all_to_all | solution.py:614
  257.7 1.9 add_convert_fusion
  261.4 2.2 collective-permute-start.8
  263.8 2.6 collective-permute-start.12
  268.1 1.9 collective-permute-start.9
  270.7 2.7 collective-permute-done.12
  275.1 13.7 %collective-permute-done.7 = bf16[48,4096]{1,0:T(8,128)(2,1)S(1)} collective-permute-done((bf16[48,4096]{1,0:T(8,128)(2,1)S(1)}, bf16[48,4096]{1,0:T(8,128)(2,1)S(1)}, u32[]{:S(2)}, u32[]{:S(2)}) %collective-permute-start.7) | collective-permute-done | bytes 393248 | tf_op jit(solution)/shard_map/ppermute | solution.py:563
  288.8 3.2 %collective-permute-done.9 = bf16[48,4096]{1,0:T(8,128)(2,1)S(1)} collective-permute-done((bf16[48,4096]{1,0:T(8,128)(2,1)S(1)}, bf16[48,4096]{1,0:T(8,128)(2,1)S(1)}, u32[]{:S(2)}, u32[]{:S(2)}) %collective-permute-start.9) | collective-permute-done | bytes 393248 | tf_op jit(solution)/shard_map/ppermute | solution.py:563
  294.4 1.7 copy-done
  296.1 3.7 %finish.1 = (f32[512,2048]{1,0:T(8,128)}, f32[512,512]{1,0:T(8,128)}) custom-call(bf16[512,2560]{1,0:T(8,128)(2,1)S(1)} %copy-done), custom_call_target="tpu_custom_call" | custom-call | tf_op jit(solution)/shard_map/finish/pallas_call | solution.py:442
  (46 shorter events, 15.6 us)
Async XLA Ops:
  34.4 56.1 %all-to-all-start.1 = ((bf16[16,256,512]{2,1,0:T(8,128)(2,1)}), bf16[16,256,512]{2,1,0:T(8,128)(2,1)}, u32[]{:S(2)}, u32[]{:S(2)}) async-start(bf16[16,256,512]{2,1,0:T(8,128)(2,1)} %bitcast.14), calls=%async_computation.1 | async-start | bytes 8388608 | tf_op jit(solution)/shard_map/all_to_all | solution.py:607
  145.6 9.2 %collective-permute-start = (bf16[256,2560]{1,0:T(8,128)(2,1)}, bf16[256,2560]{1,0:T(8,128)(2,1)}, u32[]{:S(2)}, u32[]{:S(2)}) collective-permute-start(bf16[256,2560]{1,0:T(8,128)(2,1)} %get-tuple-element.28), channel_id=1, source_target_pairs={{0,16},{16,0},{32,48},{48,32},{64,80},{80,64},{96,112},{112,96},{1... | collective-permute-start | bytes 3932168 | tf_op jit(solution)/shard_map/ppermute | solution.py:559
  150.8 45.5 %all-to-all-start.4 = ((bf16[16,256,384]{2,1,0:T(8,128)(2,1)}), bf16[16,256,384]{2,1,0:T(8,128)(2,1)S(1)}, u32[]{:S(2)}, u32[]{:S(2)}) async-start(bf16[16,256,384]{2,1,0:T(8,128)(2,1)} %bitcast.15), calls=%async_computation.4 | async-start | bytes 6291456 | tf_op jit(solution)/shard_map/all_to_all | solution.py:614
  156.9 8.1 %collective-permute-start.1 = (bf16[32,2560]{1,0:T(8,128)(2,1)S(1)}, bf16[32,2560]{1,0:T(8,128)(2,1)S(1)}, u32[]{:S(2)}, u32[]{:S(2)}) collective-permute-start(bf16[32,2560]{1,0:T(8,128)(2,1)S(1)} %get-tuple-element.44), channel_id=1, source_target_pairs={{0,32},{16,48},{32,64},{48,80},{64,96},{80,112},{96,0},{112,16},{1... | collective-permute-start | bytes 491528 | tf_op jit(solution)/shard_map/ppermute | solution.py:563
  158.6 6.4 %collective-permute-start.3 = (bf16[32,2560]{1,0:T(8,128)(2,1)S(1)}, bf16[32,2560]{1,0:T(8,128)(2,1)S(1)}, u32[]{:S(2)}, u32[]{:S(2)}) collective-permute-start(bf16[32,2560]{1,0:T(8,128)(2,1)S(1)} %get-tuple-element.45), channel_id=1, source_target_pairs={{0,96},{16,112},{32,0},{48,16},{64,32},{80,48},{96,64},{112,80},{1... | collective-permute-start | bytes 491528 | tf_op jit(solution)/shard_map/ppermute | solution.py:563
  165.1 9.7 %collective-permute-start.2 = (bf16[64,2560]{1,0:T(8,128)(2,1)S(1)}, bf16[64,2560]{1,0:T(8,128)(2,1)S(1)}, u32[]{:S(2)}, u32[]{:S(2)}) collective-permute-start(bf16[64,2560]{1,0:T(8,128)(2,1)S(1)} %pad_maximum_fusion.3), channel_id=1, source_target_pairs={{0,32},{16,48},{32,64},{48,80},{64,96},{80,112},{96,0},{112,16},{1... | collective-permute-start | bytes 983048 | tf_op jit(solution)/shard_map/ppermute | solution.py:563
  165.7 9.2 %collective-permute-start.4 = (bf16[64,2560]{1,0:T(8,128)(2,1)S(1)}, bf16[64,2560]{1,0:T(8,128)(2,1)S(1)}, u32[]{:S(2)}, u32[]{:S(2)}) collective-permute-start(bf16[64,2560]{1,0:T(8,128)(2,1)S(1)} %pad_maximum_fusion.4), channel_id=1, source_target_pairs={{0,96},{16,112},{32,0},{48,16},{64,32},{80,48},{96,64},{112,80},{1... | collective-permute-start | bytes 983048 | tf_op jit(solution)/shard_map/ppermute | solution.py:563
  178.6 29.3 %copy-start.3 = (s32[16,1,256]{2,1,0:T(1,128)S(1)}, s32[16,1,256]{2,1,0:T(1,128)}, u32[]{:S(2)}) copy-start(s32[16,1,256]{2,1,0:T(1,128)} %all_to_all.29) | copy-start | bytes 49156
  196.3 30.6 %all-to-all-start.2 = ((bf16[16,336,128]{2,1,0:T(8,128)(2,1)}), bf16[16,336,128]{2,1,0:T(8,128)(2,1)}, u32[]{:S(2)}, u32[]{:S(2)}) async-start(bf16[16,336,128]{2,1,0:T(8,128)(2,1)} %pad_maximum_fusion), calls=%async_computation.2 | async-start | bytes 2752512 | tf_op jit(solution)/shard_map/all_to_all | solution.py:614
  207.9 86.4 %all-gather.2.cloned.1.call-start = ((), (), s32[]{:S(2)}) async-start(), calls=%async_computation.5 | async-start | bytes 2949120 | tf_op jit(solution)/shard_map/all_gather | solution.py:634
  219.0 1.2 copy-start.1
  220.2 37.5 %collective-permute-start.5 = (bf16[192,4096]{1,0:T(8,128)(2,1)}, bf16[192,4096]{1,0:T(8,128)(2,1)}, u32[]{:S(2)}, u32[]{:S(2)}) collective-permute-start(bf16[192,4096]{1,0:T(8,128)(2,1)} %get-tuple-element.33), channel_id=1, source_target_pairs={{0,16},{16,0},{32,48},{48,32},{64,80},{80,64},{96,112},{112,96},{1... | collective-permute-start | bytes 4718600 | tf_op jit(solution)/shard_map/ppermute | solution.py:559
  236.4 21.2 %collective-permute-start.10 = (bf16[64,4096]{1,0:T(8,128)(2,1)S(1)}, bf16[64,4096]{1,0:T(8,128)(2,1)S(1)}, u32[]{:S(2)}, u32[]{:S(2)}) collective-permute-start(bf16[64,4096]{1,0:T(8,128)(2,1)S(1)} %get-tuple-element.35), channel_id=1, source_target_pairs={{0,16},{16,0},{32,48},{48,32},{64,80},{80,64},{96,112},{112,96},{1... | collective-permute-start | bytes 1572872 | tf_op jit(solution)/shard_map/ppermute | solution.py:559
  240.6 17.2 %copy-start.2 = (bf16[192,4096]{1,0:T(8,128)(2,1)S(1)}, bf16[192,4096]{1,0:T(8,128)(2,1)}, u32[]{:S(2)}) copy-start(bf16[192,4096]{1,0:T(8,128)(2,1)} %copy-done.1) | copy-start | bytes 4718596
  259.7 7.3 %collective-permute-start.6 = (bf16[24,4096]{1,0:T(8,128)(2,1)S(1)}, bf16[24,4096]{1,0:T(8,128)(2,1)S(1)}, u32[]{:S(2)}, u32[]{:S(2)}) collective-permute-start(bf16[24,4096]{1,0:T(8,128)(2,1)S(1)} %get-tuple-element.38), channel_id=1, source_target_pairs={{0,32},{16,48},{32,64},{48,80},{64,96},{80,112},{96,0},{112,16},{1... | collective-permute-start | bytes 589832 | tf_op jit(solution)/shard_map/ppermute | solution.py:563
  261.4 5.6 %collective-permute-start.8 = (bf16[24,4096]{1,0:T(8,128)(2,1)S(1)}, bf16[24,4096]{1,0:T(8,128)(2,1)S(1)}, u32[]{:S(2)}, u32[]{:S(2)}) collective-permute-start(bf16[24,4096]{1,0:T(8,128)(2,1)S(1)} %get-tuple-element.39), channel_id=1, source_target_pairs={{0,96},{16,112},{32,0},{48,16},{64,32},{80,48},{96,64},{112,80},{1... | collective-permute-start | bytes 589832 | tf_op jit(solution)/shard_map/ppermute | solution.py:563
  263.7 7.0 %collective-permute-start.11 = (bf16[16,4096]{1,0:T(8,128)(2,1)S(1)}, bf16[16,4096]{1,0:T(8,128)(2,1)S(1)}, u32[]{:S(2)}, u32[]{:S(2)}) collective-permute-start(bf16[16,4096]{1,0:T(8,128)(2,1)S(1)} %get-tuple-element.48), channel_id=1, source_target_pairs={{0,32},{16,48},{32,64},{48,80},{64,96},{80,112},{96,0},{112,16},{1... | collective-permute-start | bytes 393224 | tf_op jit(solution)/shard_map/ppermute | solution.py:563
  263.8 9.6 %collective-permute-start.12 = (bf16[16,4096]{1,0:T(8,128)(2,1)S(1)}, bf16[16,4096]{1,0:T(8,128)(2,1)S(1)}, u32[]{:S(2)}, u32[]{:S(2)}) collective-permute-start(bf16[16,4096]{1,0:T(8,128)(2,1)S(1)} %get-tuple-element.50), channel_id=1, source_target_pairs={{0,64},{16,80},{32,96},{48,112},{64,0},{80,16},{96,32},{112,48},{1... | collective-permute-start | bytes 393224 | tf_op jit(solution)/shard_map/ppermute | solution.py:563
  266.3 8.7 %collective-permute-start.13 = (bf16[16,4096]{1,0:T(8,128)(2,1)S(1)}, bf16[16,4096]{1,0:T(8,128)(2,1)S(1)}, u32[]{:S(2)}, u32[]{:S(2)}) collective-permute-start(bf16[16,4096]{1,0:T(8,128)(2,1)S(1)} %get-tuple-element.49), channel_id=1, source_target_pairs={{0,96},{16,112},{32,0},{48,16},{64,32},{80,48},{96,64},{112,80},{1... | collective-permute-start | bytes 393224 | tf_op jit(solution)/shard_map/ppermute | solution.py:563
  267.2 21.6 %collective-permute-start.7 = (bf16[48,4096]{1,0:T(8,128)(2,1)S(1)}, bf16[48,4096]{1,0:T(8,128)(2,1)S(1)}, u32[]{:S(2)}, u32[]{:S(2)}) collective-permute-start(bf16[48,4096]{1,0:T(8,128)(2,1)S(1)} %pad_maximum_fusion.1), channel_id=1, source_target_pairs={{0,32},{16,48},{32,64},{48,80},{64,96},{80,112},{96,0},{112,16},{1... | collective-permute-start | bytes 1179656 | tf_op jit(solution)/shard_map/ppermute | solution.py:563
  268.1 23.9 %collective-permute-start.9 = (bf16[48,4096]{1,0:T(8,128)(2,1)S(1)}, bf16[48,4096]{1,0:T(8,128)(2,1)S(1)}, u32[]{:S(2)}, u32[]{:S(2)}) collective-permute-start(bf16[48,4096]{1,0:T(8,128)(2,1)S(1)} %pad_maximum_fusion.2), channel_id=1, source_target_pairs={{0,96},{16,112},{32,0},{48,16},{64,32},{80,48},{96,64},{112,80},{1... | collective-permute-start | bytes 1179656 | tf_op jit(solution)/shard_map/ppermute | solution.py:563
  294.4 1.7 copy-start
Sparse Core Ops, SparseCore 0:
  257.7 36.6 all-gather.1
